TPU v7x, 32 devices: a whole 2x2x4 slice. The times are simulated.
32 devices in a mesh: dp: 16 (over z, y, x), tensor: 2 (over core).
Axes of the slice: x: 2, y: 2, z: 4, core: 2. Of those that a mesh axis runs over, the one named last changes fastest.
Arguments:
- layer_in: bfloat16 [8192, 768], P(('dp', 'tensor')), may hold values from -6 to 6
- norm1_gain: bfloat16 [768], P('tensor'), may hold values from 0.5 to 1.5
- qkv_weight: bfloat16 [768, 2304], P('tensor'), may hold values from -0.21875 to 0.21875
- out_weight: bfloat16 [768, 768], P('tensor'), may hold values from -4 to 4
- norm2_gain: bfloat16 [768], P('tensor'), may hold values from 0.5 to 1.5
- mlp_weight: bfloat16 [3, 768, 1152], P(None, None, 'tensor'), may hold values from -0.21875 to 0.21875
- cotangent: bfloat16 [8192, 768], P(('dp', 'tensor')), may hold values from -6 to 6
Outputs:
- layer_out: bfloat16 [8192, 768], P(('dp', 'tensor'))
- input_grad: float32 [8192, 768], P(('dp', 'tensor'))
- norm1_grad: float32 [768], P('tensor')
- qkv_grad: float32 [768, 2304], P('tensor')
- out_grad: float32 [768, 768], P('tensor')
- norm2_grad: float32 [768], P('tensor')
- mlp_grad: float32 [3, 768, 1152], P(None, None, 'tensor')
All inputs are finite; a program needn't handle non-finite values.
Results may differ from a plain program's by a relative error of at most 0.023.
Values may be sent and summed in bfloat16 or wider, within the bound.
A program may use at most 128 MiB of HBM per device.

v0:
```python
import jax
import jax.numpy as jnp
from jax import lax
from jax.sharding import PartitionSpec as P

HEADS = 12
HEAD_DIM = 64
SEQ = 512


EPS = 1e-05
THETA = 160000.0


def swapped(value, axis, distance):
    mask = 2**distance
    pairs = [(source, source ^ mask) for source in range(lax.axis_size(axis))]
    return lax.ppermute(value, axis, pairs)


def rope_tables(positions):
    half = HEAD_DIM // 2
    freq = THETA ** (-jnp.arange(half).astype(jnp.float32) * 2.0 / HEAD_DIM)
    angle = positions.astype(jnp.float32)[:, None] * freq[None, :]
    return (jnp.cos(angle)[:, None, :], jnp.sin(angle)[:, None, :])


def rotate(values, cosine, sine):
    half = HEAD_DIM // 2
    first, second = (values[..., :half], values[..., half:])
    return jnp.concatenate([first * cosine - second * sine, second * cosine + first * sine], -1)


def unrotate(values, cosine, sine):
    half = HEAD_DIM // 2
    first, second = (values[..., :half], values[..., half:])
    return jnp.concatenate([first * cosine + second * sine, second * cosine - first * sine], -1)


def layer_norm_forward(values, gain):
    centred = values - jnp.mean(values, -1, keepdims=True)
    inverse = lax.rsqrt(jnp.mean(centred * centred, -1, keepdims=True) + EPS)
    normed = centred * inverse
    return (normed * gain, normed, inverse)


def layer_norm_backward(upstream, normed, inverse, gain):
    scaled = upstream * gain
    back = inverse * (
        scaled
        - jnp.mean(scaled, -1, keepdims=True)
        - normed * jnp.mean(scaled * normed, -1, keepdims=True)
    )
    return (back, jnp.sum(upstream * normed, 0))


def gelu_parts(values):
    cdf = 0.5 * (1.0 + jax.scipy.special.erf(values * 0.7071067811865476))
    density = jnp.exp(-0.5 * values * values) * 0.3989422804014327
    return (values * cdf, cdf + values * density)


def right_product(left, weight):
    return lax.dot_general(
        left, weight, (((1,), (1,)), ((), ())), preferred_element_type=jnp.float32
    )


def left_product(left, right):
    return lax.dot_general(
        left, right, (((0,), (0,)), ((), ())), preferred_element_type=jnp.float32
    )


def collect_keys(key_own, value_own, position_slot):
    pair = (key_own, value_own)
    far_key, far_value = swapped((pair[0], pair[1]), "tensor", 0)
    upper = (position_slot >> 0) % 2 == 1
    pair = (
        jnp.where(
            upper, jnp.concatenate([far_key, pair[0]], 0), jnp.concatenate([pair[0], far_key], 0)
        ),
        jnp.where(
            upper,
            jnp.concatenate([far_value, pair[1]], 0),
            jnp.concatenate([pair[1], far_value], 0),
        ),
    )
    return pair


def return_grads(key_grad, value_grad, position_slot):
    pair = (key_grad, value_grad)
    middle = pair[0].shape[0] // 2
    upper = (position_slot >> 0) % 2 == 1
    keep_key = jnp.where(upper, pair[0][middle:], pair[0][:middle])
    send_key = jnp.where(upper, pair[0][:middle], pair[0][middle:])
    keep_value = jnp.where(upper, pair[1][middle:], pair[1][:middle])
    send_value = jnp.where(upper, pair[1][:middle], pair[1][middle:])
    back_key = swapped(send_key.astype(jnp.bfloat16), "tensor", 0).astype(send_key.dtype)
    back_value = swapped(send_value.astype(jnp.bfloat16), "tensor", 0).astype(send_value.dtype)
    pair = (keep_key + back_key, keep_value + back_value)
    return pair


def body(layer_in, norm1_gain, qkv_weight, out_weight, norm2_gain, mlp_weight, cotangent):
    f32 = jnp.float32
    bf16 = jnp.bfloat16
    rows = layer_in.shape[0]
    width = layer_in.shape[1]
    span = SEQ // rows
    scale = HEAD_DIM ** (-0.5)
    first_norm_gain, second_norm_gain, w_qkv, w_out = (
        lax.all_gather(norm1_gain, "tensor", axis=0, tiled=True),
        lax.all_gather(norm2_gain, "tensor", axis=0, tiled=True),
        lax.all_gather(qkv_weight, "tensor", axis=0, tiled=True),
        lax.all_gather(out_weight, "tensor", axis=0, tiled=True),
    )
    first_norm_gain = first_norm_gain.astype(f32)
    second_norm_gain = second_norm_gain.astype(f32)
    position_slot = lax.axis_index("tensor") % span
    cosine, sine = rope_tables(position_slot * rows + jnp.arange(rows, dtype=jnp.int32))
    input_float_rows = layer_in.astype(f32)
    first_normed_rows, standardized_first, inverse_deviation_first = layer_norm_forward(
        input_float_rows, first_norm_gain
    )
    h1 = first_normed_rows.astype(bf16)
    qkv = jnp.dot(h1, w_qkv, preferred_element_type=f32)
    query = rotate(qkv[:, :width].reshape(rows, HEADS, HEAD_DIM), cosine, sine).astype(bf16)
    key_own = (
        rotate(qkv[:, width : 2 * width].reshape(rows, HEADS, HEAD_DIM), cosine, sine)
        .astype(bf16)
        .reshape(rows, width)
    )
    value_own = qkv[:, 2 * width :].astype(bf16)
    key_all, value_all = collect_keys(key_own, value_own, position_slot)
    keys = key_all.reshape(SEQ, HEADS, HEAD_DIM)
    values = value_all.reshape(SEQ, HEADS, HEAD_DIM)
    scores = jnp.einsum("qhd,khd->hqk", query, keys, preferred_element_type=f32) * scale
    total = jnp.log(jnp.sum(jnp.exp(scores), -1))
    probs_b = jnp.exp(scores - total[..., None]).astype(bf16)
    attended = (
        jnp.einsum("hqk,khd->qhd", probs_b, values, preferred_element_type=f32)
        .astype(bf16)
        .reshape(rows, width)
    )
    attention_mixed = input_float_rows + jnp.dot(attended, w_out, preferred_element_type=f32)
    second_normed_rows, standardized_second, inverse_deviation_second = layer_norm_forward(
        attention_mixed, second_norm_gain
    )
    h2 = second_normed_rows.astype(bf16)
    dz_f = cotangent.astype(f32)
    group = lax.all_gather(h2, "tensor", axis=0, tiled=True)
    gate_pre = jnp.dot(group, mlp_weight[0], preferred_element_type=f32)
    up_pre = jnp.dot(group, mlp_weight[1], preferred_element_type=f32)
    gel, slope = gelu_parts(gate_pre)
    hidden = (gel * up_pre).astype(bf16)
    branch = lax.psum_scatter(
        right_product(hidden, mlp_weight[2]).astype(jnp.bfloat16),
        "tensor",
        scatter_dimension=0,
        tiled=True,
    ).astype(jnp.float32)
    layer_out = (attention_mixed + branch).astype(bf16)
    grad_group = lax.all_gather(cotangent, "tensor", axis=0, tiled=True)
    grad_hidden = jnp.dot(grad_group, mlp_weight[2], preferred_element_type=f32)
    grad_gate = (grad_hidden * up_pre * slope).astype(bf16)
    grad_up = (grad_hidden * gel).astype(bf16)
    grad_mlp = jnp.stack(
        [
            left_product(group, grad_gate),
            left_product(group, grad_up),
            left_product(grad_group, hidden),
        ]
    )
    gradient_hidden_second = lax.psum_scatter(
        right_product(grad_gate, mlp_weight[0]) + right_product(grad_up, mlp_weight[1]),
        "tensor",
        scatter_dimension=0,
        tiled=True,
    )
    second_norm_backward, gradient_gain_second = layer_norm_backward(
        gradient_hidden_second, standardized_second, inverse_deviation_second, second_norm_gain
    )
    grad_mixed = dz_f + second_norm_backward
    grad_mixed_b = grad_mixed.astype(bf16)
    grad_wout = left_product(attended, grad_mixed_b)
    grad_att = right_product(grad_mixed_b, w_out).astype(bf16).reshape(rows, HEADS, HEAD_DIM)
    scores = jnp.einsum("qhd,khd->hqk", query, keys, preferred_element_type=f32) * scale
    probs = jnp.exp(scores - total[..., None])
    probs_b = probs.astype(bf16)
    grad_probs = jnp.einsum("qhd,khd->hqk", grad_att, values, preferred_element_type=f32)
    delta = jnp.einsum(
        "qhd,qhd->hq", grad_att.astype(f32), attended.reshape(rows, HEADS, HEAD_DIM).astype(f32)
    )
    grad_scores = (probs * (grad_probs - delta[..., None])).astype(bf16)
    grad_query = jnp.einsum("hqk,khd->qhd", grad_scores, keys, preferred_element_type=f32) * scale
    grad_keys = jnp.einsum("hqk,qhd->khd", grad_scores, query, preferred_element_type=f32) * scale
    grad_values = jnp.einsum("hqk,qhd->khd", probs_b, grad_att, preferred_element_type=f32)
    key_total, value_total = return_grads(
        grad_keys.reshape(SEQ, width), grad_values.reshape(SEQ, width), position_slot
    )
    grad_q = unrotate(grad_query, cosine, sine).reshape(rows, width)
    grad_k = unrotate(key_total.reshape(rows, HEADS, HEAD_DIM), cosine, sine).reshape(rows, width)
    grad_qkv = jnp.concatenate([grad_q, grad_k, value_total], 1).astype(bf16)
    grad_wqkv = left_product(h1, grad_qkv)
    gradient_hidden_first = right_product(grad_qkv, w_qkv)
    first_norm_backward, gradient_gain_first = layer_norm_backward(
        gradient_hidden_first, standardized_first, inverse_deviation_first, first_norm_gain
    )
    input_grad = grad_mixed + first_norm_backward
    shares = (
        lax.psum_scatter(
            grad_wqkv.astype(jnp.bfloat16), "tensor", scatter_dimension=0, tiled=True
        ).astype(jnp.float32),
        lax.psum_scatter(
            grad_wout.astype(jnp.bfloat16), "tensor", scatter_dimension=0, tiled=True
        ).astype(jnp.float32),
        lax.psum_scatter(
            gradient_gain_first.astype(jnp.bfloat16), "tensor", scatter_dimension=0, tiled=True
        ).astype(jnp.float32),
        lax.psum_scatter(
            gradient_gain_second.astype(jnp.bfloat16), "tensor", scatter_dimension=0, tiled=True
        ).astype(jnp.float32),
    )
    totals = (
        lax.psum(shares[0].astype(jnp.bfloat16), "dp").astype(jnp.float32),
        lax.psum(shares[1].astype(jnp.bfloat16), "dp").astype(jnp.float32),
        lax.psum(shares[2].astype(jnp.bfloat16), "dp").astype(jnp.float32),
        lax.psum(shares[3].astype(jnp.bfloat16), "dp").astype(jnp.float32),
        lax.psum(grad_mlp.astype(jnp.bfloat16), "dp").astype(jnp.float32),
    )
    return (layer_out, input_grad, totals[2], totals[0], totals[1], totals[3], totals[4])


def solution(mesh):
    return jax.shard_map(
        body,
        mesh=mesh,
        in_specs=(
            P(("dp", "tensor"), None),
            P("tensor"),
            P("tensor", None),
            P("tensor", None),
            P("tensor"),
            P(None, None, "tensor"),
            P(("dp", "tensor"), None),
        ),
        out_specs=(
            P(("dp", "tensor"), None),
            P(("dp", "tensor"), None),
            P("tensor"),
            P("tensor", None),
            P("tensor", None),
            P("tensor"),
            P(None, None, "tensor"),
        ),
        check_vma=False,
    )
```

profile of v0, /device:TPU:0, one launch (start us, length us, event | category | flops | bytes accessed | tf_op | source)
XLA Modules:
  0.0 339.7 jit_solution(17604484921782706955)
XLA Ops:
  7.2 0.7 all-gather.5.cloned.1.call-update
  8.0 0.7 all-gather.7.cloned.1.call-update
  8.8 2.0 all-gather
  11.3 1.8 all-gather.1
  13.1 0.8 multiply_cosine_fusion
  14.0 11.1 %all-gather.5.cloned.1.call-done = bf16[768,2304]{1,0:T(8,128)(2,1)} async-done(((bf16[384,2304]{1,0:T(8,128)(2,1)}), bf16[768,2304]{1,0:T(8,128)(2,1)}) %all-gather.5.cloned.1.call-update) | async-done | bytes 3538960 | tf_op jit(solution)/shard_map/all_gather | solution.py:116
  25.0 3.1 fusion.89
  28.2 1.2 fusion.91
  29.4 1.4 copy.32
  30.8 0.9 multiply_subtract_fusion
  31.8 0.8 slice.148
  33.2 2.5 all_gather.23
  35.7 1.2 copy.30
  37.3 1.3 copy.29
  38.6 4.9 %fusion.71 = f32[12,256,512]{2,1,0:T(8,128)} fusion(bf16[256,12,32]{0,2,1:T(8,128)(2,1)S(1)} %get-tuple-element.32, bf16[256,12,32]{0,2,1:T(8,128)(2,1)S(1)} %get-tuple-element.31, bf16[256,12,64]{0,2,1:T(8,128)(2,1)S(1)} %maximum_convert_fusion, bf16[256,12,64]{0,2,1:T(8,128)(2,1)} %bitcast.7, pred[]{:T(512)S(6)} %eq.8), kind=kOutput, calls=%fused_computation.109 | convolution fusion | flops 205651968 | bytes 7471105 | tf_op jit(solution)/shard_map/qhd,khd->hqk/dot_general | solution.py:139
  43.6 7.0 %fusion.18 = bf16[12,64,256]{2,1,0:T(8,128)(2,1)S(1)} fusion(f32[12,256,512]{2,1,0:T(8,128)} %fusion.71, bf16[256,12,64]{0,2,1:T(8,128)(2,1)S(1)} %bitcast.91, bf16[256,12,64]{0,2,1:T(8,128)(2,1)S(1)} %bitcast.93, pred[]{:T(512)S(6)} %eq.8), kind=kOutput, calls=%fused_computation.29 | convolution fusion | flops 211357184 | bytes 7471105 | tf_op jit(solution)/shard_map/hqk,khd->qhd/dot_general | solution.py:143
  50.6 1.9 fusion.92
  52.9 2.5 all_gather.22
  55.4 0.7 fusion.49
  56.3 0.7 fusion.45
  56.9 0.5 copy-done.23
  57.4 1.1 multiply_convert_fusion.1
  58.6 0.8 fusion.47
  59.4 2.0 convolution_add_fusion
  61.5 2.9 convolution_convert_fusion.5
  64.6 7.2 %fusion.1 = f32[12,256,512]{2,1,0:T(8,128)} fusion(bf16[256,12,32]{0,2,1:T(8,128)(2,1)S(1)} %get-tuple-element.32, bf16[256,12,32]{0,2,1:T(8,128)(2,1)S(1)} %get-tuple-element.31, bf16[256,12,64]{0,2,1:T(8,128)(2,1)S(1)} %maximum_convert_fusion, bf16[256,12,64]{0,2,1:T(8,128)(2,1)} %bitcast.7, pred[]{:T(512)S(6)} %eq.8), kind=kOutput, calls=%fused_computation.2 | convolution fusion | flops 416026112 | bytes 7471105 | tf_op jit(solution)/shard_map/reduce_sum | solution.py:140
  71.8 2.2 multiply_reduce_fusion
  74.0 0.6 broadcast_multiply_fusion.2
  74.6 9.4 %reduce-scatter.5.cloned.1.call-done = bf16[256,768]{1,0:T(8,128)(2,1)} async-done(((bf16[512,768]{1,0:T(8,128)(2,1)}), bf16[256,768]{1,0:T(8,128)(2,1)}) %reduce-scatter.5.cloned.1.call-update) | async-done | bytes 393232 | tf_op jit(solution)/shard_map/reduce_scatter | solution.py:158
  83.9 2.1 multiply_add_fusion
  86.0 1.5 convolution_convert_fusion.1
  87.5 0.4 copy-done.6
  87.9 0.5 convolution_convert_fusion.6
  88.6 8.0 %fusion.11 = f32[512,12,64]{0,2,1:T(8,128)} fusion(bf16[256,12,64]{0,2,1:T(8,128)(2,1)S(1)} %bitcast.84, f32[12,256,512]{2,1,0:T(8,128)} %fusion.71), kind=kOutput, calls=%fused_computation.18 | convolution fusion | flops 207621632 | bytes 8257536 | tf_op jit(solution)/shard_map/hqk,qhd->khd/dot_general | solution.py:199
  96.7 4.6 %multiply_convert_fusion = bf16[12,256,512]{2,1,0:T(8,128)(2,1)S(1)} fusion(f32[12,256,512]{2,1,0:T(8,128)} %fusion.1, f32[12,256]{1,0:T(8,128)S(1)} %fusion.59, bf16[256,12,64]{0,2,1:T(8,128)(2,1)} %bitcast.86, bf16[256,12,64]{0,2,1:T(8,128)(2,1)} %bitcast.92, bf16[256,12,64]{0,2,1:T(8,128)(2,1)} %bitcast.94, pred[]{:T(512)S(6)} %eq.8), kind=kOutput, calls=%fused_computation.3 | convolution fusion | flops 209584128 | bytes 10629121 | tf_op jit(solution)/shard_map/qhd,khd->hqk/dot_general | solution.py:192
  101.3 0.7 multiply_bitcast_fusion
  102.0 1.1 copy-done.3
  103.1 0.8 select_convert_fusion.1
  104.2 1.6 slice_select_fusion.1
  106.3 0.4 collective-permute-start.3
  106.7 0.4 copy-done.20
  107.1 2.2 fusion.17
  109.4 1.1 bitcast_add_fusion.1
  111.0 0.7 copy-done.32
  111.7 3.1 convolution_convert_fusion
  115.1 0.8 copy-done.24
  115.9 1.7 fusion.14
  117.6 0.6 fusion.16
  118.3 0.4 copy-done.41
  118.7 0.6 fusion.15
  119.3 1.8 pad_maximum_fusion
  121.1 8.7 %reduce-scatter.9.cloned.1.call-done = bf16[384,2304]{1,0:T(8,128)(2,1)} async-done(((bf16[768,2304]{1,0:T(8,128)(2,1)}), bf16[384,2304]{1,0:T(8,128)(2,1)}) %reduce-scatter.9.cloned.1.call-update) | async-done | bytes 1769488 | tf_op jit(solution)/shard_map/reduce_scatter | solution.py:213
  129.8 0.6 copy-done.42
  130.5 0.6 dynamic-slice
  131.7 3.4 %fusion.56 = (bf16[768]{0:T(1024)(128)(2,1)S(1)}, f32[256]{0:T(256)S(1)}, f32[256]{0:T(256)S(1)}, f32[256,768]{1,0:T(8,128)S(1)}) fusion(bf16[256,768]{1,0:T(8,128)(2,1)S(1)} %copy-done.2, f32[256]{0:T(256)S(1)} %copy-done.36, f32[256]{0:T(256)S(1)} %broadcast_multiply_fusion.5, f32[768]{0:T(1024)S(1)} %reshape.182, ...), kind=kOutput, calls=%fused_computation.64 | convolution fusion | flops 911276800 | bytes 5906944 | tf_op jit(solution)/shard_map/dot_general | solution.py:64
  135.2 2.5 all-reduce.4
  137.8 44.4 %all-reduce.2 = (bf16[384]{0:T(512)(128)(2,1)S(1)}, bf16[384]{0:T(512)(128)(2,1)S(1)}) all-reduce(bf16[384]{0:T(512)(128)(2,1)S(1)} %dynamic-slice.1, bf16[384]{0:T(512)(128)(2,1)S(1)} %dynamic-slice.3), channel_id=1, replica_groups=mesh['dp'=16,'tensor'=2] {'dp'}, use_global_device_ids=true, to_apply=%region_13.14 | all-reduce | flops 768 | bytes 3072 | tf_op jit(solution)/shard_map/psum | solution.py:229
  182.2 0.6 convert_element_type.165
  182.8 0.6 convert_element_type.171
  183.4 1.2 fusion.55
  184.6 140.7 %all-reduce.7.cloned.1.call-done = (bf16[384,2304]{1,0:T(8,128)(2,1)}, bf16[384,768]{1,0:T(8,128)(2,1)}, bf16[3,768,576]{1,2,0:T(8,128)(2,1)}) async-done(((bf16[384,2304]{1,0:T(8,128)(2,1)}, bf16[384,768]{1,0:T(8,128)(2,1)}, bf16[3,768,576]{1,2,0:T(8,128)(2,1)}), (bf16[384,2304]{1,0:T(8,128)(2,1)}, bf16[384,768]{1,0:T(8,128)(2,1)}, bf16[3,768,576]{1,2,0:T(8,128)(2,1)})) %all-reduce.7.cloned.1.call-update) | async-done | bytes 5013520 | tf_op jit(solution)/shard_map/psum | solution.py:227
  325.3 3.6 %convert_element_type.167 = f32[384,2304]{1,0:T(8,128)} convert(bf16[384,2304]{1,0:T(8,128)(2,1)} %get-tuple-element.15) | non-fusion elementwise | flops 884736 | bytes 5308416 | tf_op jit(solution)/shard_map/convert_element_type | solution.py:227
  328.9 1.1 convert_element_type.169
  330.0 2.8 convert_element_type.172
  (133 shorter events, 4.5 us)
Async XLA Ops:
  7.2 1.6 copy-start.38
  7.2 3.6 %copy-start.2 = (bf16[256,768]{1,0:T(8,128)(2,1)S(1)}, bf16[256,768]{1,0:T(8,128)(2,1)}, u32[]{:S(2)}) copy-start(bf16[256,768]{1,0:T(8,128)(2,1)} %param.7) | copy-start | bytes 1179652
  7.2 4.1 %copy-start.39 = (bf16[384]{0:T(512)(128)(2,1)S(1)}, bf16[384]{0:T(512)(128)(2,1)}, u32[]{:S(2)}) copy-start(bf16[384]{0:T(512)(128)(2,1)} %param.11) | copy-start | bytes 2308
  7.2 17.8 %all-gather.5.cloned.1.call-start = ((), (), s32[]{:S(2)}) async-start(), calls=%async_computation.4 | async-start | bytes 5308416 | tf_op jit(solution)/shard_map/all_gather | solution.py:116
  7.9 42.7 %all-gather.7.cloned.1.call-start = ((), (), s32[]{:S(2)}) async-start(), calls=%async_computation.5 | async-start | bytes 1769472 | tf_op jit(solution)/shard_map/all_gather | solution.py:117
  8.7 63.1 %reduce-scatter.7.cloned.1.call-start = ((), (), s32[]{:S(2)}) async-start(), calls=%async_computation.7 | async-start | bytes 2359296 | tf_op jit(solution)/shard_map/reduce_scatter | solution.py:176
  11.2 17.0 %copy-start.35 = (f32[256]{0:T(256)}, f32[256]{0:T(256)S(1)}, u32[]{:S(2)}) copy-start(f32[256]{0:T(256)S(1)} %add_rsqrt_fusion.1) | copy-start | bytes 3076
  30.8 2.4 copy-start.17
  31.8 5.1 %copy-start.10 = (f32[256,768]{1,0:T(8,128)S(1)}, f32[256,768]{1,0:T(8,128)}, u32[]{:S(2)}) copy-start(f32[256,768]{1,0:T(8,128)} %get-tuple-element.24) | copy-start | bytes 2359300
  32.6 32.0 %copy-start.19 = (bf16[256,12,64]{0,2,1:T(8,128)(2,1)}, bf16[256,12,64]{0,2,1:T(8,128)(2,1)S(1)}, u32[]{:S(2)}) copy-start(bf16[256,12,64]{0,2,1:T(8,128)(2,1)S(1)} %maximum_convert_fusion) | copy-start | bytes 1179652
  32.6 4.6 %copy-start.28 = (f32[256,32]{0,1:T(8,128)S(1)}, f32[256,32]{0,1:T(8,128)}, u32[]{:S(2)}) copy-start(f32[256,32]{0,1:T(8,128)} %get-tuple-element.37) | copy-start | bytes 98308
  32.6 4.6 %copy-start.30 = (f32[256,32]{0,1:T(8,128)S(1)}, f32[256,32]{0,1:T(8,128)}, u32[]{:S(2)}) copy-start(f32[256,32]{0,1:T(8,128)} %get-tuple-element.38) | copy-start | bytes 98308
  32.6 6.0 %collective-permute-start.1 = (bf16[256,768]{0,1:T(8,128)(2,1)S(1)}, bf16[256,768]{0,1:T(8,128)(2,1)}, u32[]{:S(2)}, u32[]{:S(2)}) collective-permute-start(bf16[256,768]{0,1:T(8,128)(2,1)S(1)} %bitcast.90), channel_id=1, source_target_pairs={{0,1},{1,0},{2,3},{3,2},{4,5},{5,4},{6,7},{7,6},{8,9},{9,8},{10,11... | collective-permute-start | bytes 1179656 | tf_op jit(solution)/shard_map/ppermute | solution.py:18
  32.9 4.4 %collective-permute-start = (bf16[256,768]{1,0:T(8,128)(2,1)}, bf16[256,768]{1,0:T(8,128)(2,1)}, u32[]{:S(2)}, u32[]{:S(2)}) collective-permute-start(bf16[256,768]{1,0:T(8,128)(2,1)} %slice.148), channel_id=1, source_target_pairs={{0,1},{1,0},{2,3},{3,2},{4,5},{5,4},{6,7},{7,6},{8,9},{9,8},{10,11... | collective-permute-start | bytes 1179656 | tf_op jit(solution)/shard_map/ppermute | solution.py:18
  36.9 6.7 %copy-start.21 = (bf16[256,768]{0,1:T(8,128)(2,1)}, bf16[256,768]{0,1:T(8,128)(2,1)S(1)}, u32[]{:S(2)}) copy-start(bf16[256,768]{0,1:T(8,128)(2,1)S(1)} %copy.30) | copy-start | bytes 1179652
  37.3 27.3 %copy-start.13 = (bf16[256,12,32]{0,2,1:T(8,128)(2,1)}, bf16[256,12,32]{0,2,1:T(8,128)(2,1)S(1)}, u32[]{:S(2)}) copy-start(bf16[256,12,32]{0,2,1:T(8,128)(2,1)S(1)} %get-tuple-element.31) | copy-start | bytes 589828
  37.3 27.3 %copy-start.15 = (bf16[256,12,32]{0,2,1:T(8,128)(2,1)}, bf16[256,12,32]{0,2,1:T(8,128)(2,1)S(1)}, u32[]{:S(2)}) copy-start(bf16[256,12,32]{0,2,1:T(8,128)(2,1)S(1)} %get-tuple-element.32) | copy-start | bytes 589828
  38.6 5.0 %copy-start.22 = (bf16[256,768]{0,1:T(8,128)(2,1)}, bf16[256,768]{0,1:T(8,128)(2,1)S(1)}, u32[]{:S(2)}) copy-start(bf16[256,768]{0,1:T(8,128)(2,1)S(1)} %copy.29) | copy-start | bytes 1179652
  52.5 2.9 copy-start.11
  52.7 3.4 copy-start.34
  55.4 0.9 copy-start.4
  56.3 1.1 copy-start.23
  58.6 0.8 copy-start.25
  58.6 2.8 copy-start.40
  58.6 2.9 copy-start.43
  61.4 22.5 %reduce-scatter.5.cloned.1.call-start = ((), (), s32[]{:S(2)}) async-start(), calls=%async_computation.6 | async-start | bytes 1179648 | tf_op jit(solution)/shard_map/reduce_scatter | solution.py:158
  64.3 56.8 %reduce-scatter.11.cloned.1.call-start = ((), (), s32[]{:S(2)}) async-start(), calls=%async_computation.9 | async-start | bytes 1769472 | tf_op jit(solution)/shard_map/reduce_scatter | solution.py:216
  71.8 12.1 %copy-start.18 = (bf16[256,768]{1,0:T(8,128)(2,1)S(1)}, bf16[256,768]{1,0:T(8,128)(2,1)}, u32[]{:S(2)}) copy-start(bf16[256,768]{1,0:T(8,128)(2,1)} %param.13) | copy-start | bytes 1179652
  71.8 12.1 %copy-start.9 = (f32[256,768]{1,0:T(8,128)S(1)}, f32[256,768]{1,0:T(8,128)}, u32[]{:S(2)}) copy-start(f32[256,768]{1,0:T(8,128)} %reduce-scatter.7.cloned.1.call-done) | copy-start | bytes 2359300
  86.0 2.4 copy-start
  86.0 1.9 copy-start.6
  88.6 8.0 %copy-start.8 = (bf16[256,768]{0,1:T(8,128)(2,1)}, bf16[256,768]{0,1:T(8,128)(2,1)S(1)}, u32[]{:S(2)}) copy-start(bf16[256,768]{0,1:T(8,128)(2,1)S(1)} %copy.33) | copy-start | bytes 1179652
  96.7 4.6 %copy-start.14 = (bf16[256,12,32]{0,2,1:T(8,128)(2,1)S(1)}, bf16[256,12,32]{0,2,1:T(8,128)(2,1)}, u32[]{:S(2)}) copy-start(bf16[256,12,32]{0,2,1:T(8,128)(2,1)} %copy-done.13) | copy-start | bytes 589828
  96.7 4.6 %copy-start.16 = (bf16[256,12,32]{0,2,1:T(8,128)(2,1)S(1)}, bf16[256,12,32]{0,2,1:T(8,128)(2,1)}, u32[]{:S(2)}) copy-start(bf16[256,12,32]{0,2,1:T(8,128)(2,1)} %copy-done.15) | copy-start | bytes 589828
  102.0 1.1 copy-start.3
  104.0 5.4 %collective-permute-start.2 = (bf16[256,768]{0,1:T(8,128)(2,1)}, bf16[256,768]{0,1:T(8,128)(2,1)}, u32[]{:S(2)}, u32[]{:S(2)}) collective-permute-start(bf16[256,768]{0,1:T(8,128)(2,1)} %bitcast.21), channel_id=1, source_target_pairs={{0,1},{1,0},{2,3},{3,2},{4,5},{5,4},{6,7},{7,6},{8,9},{9,8},{10,11... | collective-permute-start | bytes 1179656 | tf_op jit(solution)/shard_map/ppermute | solution.py:18
  104.2 25.6 %reduce-scatter.9.cloned.1.call-start = ((), (), s32[]{:S(2)}) async-start(), calls=%async_computation.8 | async-start | bytes 5308416 | tf_op jit(solution)/shard_map/reduce_scatter | solution.py:213
  104.2 1.9 copy-start.7
  106.1 1.0 copy-start.20
  106.3 4.5 %collective-permute-start.3 = (bf16[256,768]{0,1:T(8,128)(2,1)S(1)}, bf16[256,768]{0,1:T(8,128)(2,1)S(1)}, u32[]{:S(2)}, u32[]{:S(2)}) collective-permute-start(bf16[256,768]{0,1:T(8,128)(2,1)S(1)} %bitcast.99), channel_id=1, source_target_pairs={{0,1},{1,0},{2,3},{3,2},{4,5},{5,4},{6,7},{7,6},{8,9},{9,8},{10,11... | collective-permute-start | bytes 1179656 | tf_op jit(solution)/shard_map/ppermute | solution.py:18
  109.3 1.2 copy-start.29
  109.3 1.2 copy-start.31
  110.8 0.9 copy-start.36
  111.0 0.7 copy-start.32
  114.8 1.1 copy-start.24
  114.8 2.8 copy-start.5
  114.8 2.8 copy-start.26
  114.8 210.4 %all-reduce.7.cloned.1.call-start = ((), (), s32[]{:S(2)}) async-start(), calls=%async_computation.10 | async-start | bytes 10027008 | tf_op jit(solution)/shard_map/psum | solution.py:227
  117.6 1.1 copy-start.41
  129.8 0.7 copy-start.42
  129.8 1.9 copy-start.33
  131.7 3.4 %copy-start.37 = (bf16[768]{0:T(1024)(128)(2,1)S(1)}, bf16[768]{0:T(1024)(128)(2,1)}, u32[]{:S(2)}) copy-start(bf16[768]{0:T(1024)(128)(2,1)} %get-tuple-element.7) | copy-start | bytes 4612
  131.7 51.7 %copy-start.1 = (f32[256,768]{1,0:T(8,128)S(1)}, f32[256,768]{1,0:T(8,128)}, u32[]{:S(2)}) copy-start(f32[256,768]{1,0:T(8,128)} %copy-done) | copy-start | bytes 2359300
  325.3 3.7 %copy-start.27 = (bf16[384,768]{1,0:T(8,128)(2,1)S(1)}, bf16[384,768]{1,0:T(8,128)(2,1)}, u32[]{:S(2)}) copy-start(bf16[384,768]{1,0:T(8,128)(2,1)} %get-tuple-element.16) | copy-start | bytes 1769476
  325.3 4.7 %copy-start.12 = (bf16[3,768,576]{1,2,0:T(8,128)(2,1)S(1)}, bf16[3,768,576]{1,2,0:T(8,128)(2,1)}, u32[]{:S(2)}) copy-start(bf16[3,768,576]{1,2,0:T(8,128)(2,1)} %get-tuple-element.17) | copy-start | bytes 7962628
Sparse Core Ops, SparseCore 0:
  9.5 15.4 all-gather.4
  26.5 10.4 all-gather.6
  61.5 10.2 reduce-scatter.6
  74.4 9.4 reduce-scatter.4
  104.3 9.7 reduce-scatter.10
  116.8 12.9 reduce-scatter.8
  136.7 188.5 all-reduce.6
where the time goes:
time: 341 us; the launch traced here: 340 us
  waiting for transfers between devices  171 us (50%)
  matrix products  59 us (17%)
  blocking collectives  55.7 us (16%)
  other arithmetic  23.5 us (7%)
  between operations  15.6 us (5%)
  local copies, waits for them, and re-layouts  12.8 us (4%)
    psum x1, waiting for transfers between devices, body(): lax.psum(shares[0].astype(jnp.bfloat16), 'dp').astype(jnp.float32)  141 us
    psum x1, blocking collectives, body(): lax.psum(shares[2].astype(jnp.bfloat16), 'dp').astype(jnp.float32)  44.4 us
    all_gather x1, waiting for transfers between devices, body(): lax.all_gather(qkv_weight, 'tensor', axis=0, tiled=True)  11.1 us
    dot_general x5, matrix products, right_product(): lax.dot_general(left, weight, (((1,), (1,)), ((), ())), preferred_element...  9.54 us
    reduce_scatter x1, waiting for transfers between devices, body(): lax.psum_scatter(right_product(hidden, mlp_weight[2]).astype(jnp.bfloat16...  9.36 us
    reduce_scatter x1, waiting for transfers between devices, body(): lax.psum_scatter(grad_wqkv.astype(jnp.bfloat16), 'tensor', scatter_dimens...  8.69 us
    dot_general x1, matrix products, body(): jnp.einsum('hqk,qhd->khd', probs_b, grad_att, preferred_element_type=f32)  7.95 us
    dot_general x5, matrix products, left_product(): lax.dot_general(left, right, (((0,), (0,)), ((), ())), preferred_element_...  7.5 us
  transfers between devices with their start and end apart: 11, of which 4 were waited for; matrix products, arithmetic and copies ran while one was open for 17% of the time, Pallas kernels for 0%

commit v1 on v0

--- a/solution.py
+++ b/solution.py
@@ -1,6 +1,8 @@
 import jax
 import jax.numpy as jnp
 from jax import lax
+from jax.experimental import pallas as pl
+from jax.experimental.pallas import tpu as pltpu
 from jax.sharding import PartitionSpec as P
 
 HEADS = 12
@@ -103,6 +105,273 @@
     return pair
 
 
+def bit_count(size):
+    return size.bit_length() - 1
+
+
+def gather_rows(value, axis):
+    index = lax.axis_index(axis)
+    for distance in range(bit_count(lax.axis_size(axis))):
+        other = swapped(value, axis, distance)
+        upper = (index >> distance) % 2 == 1
+        value = jnp.where(
+            upper, jnp.concatenate([other, value], 0), jnp.concatenate([value, other], 0)
+        )
+    return value
+
+
+def scatter_sum(value, axis, wire):
+    index = lax.axis_index(axis)
+    for distance in reversed(range(bit_count(lax.axis_size(axis)))):
+        middle = value.shape[0] // 2
+        upper = (index >> distance) % 2 == 1
+        keep = jnp.where(upper, value[middle:], value[:middle])
+        send = jnp.where(upper, value[:middle], value[middle:])
+        value = keep + swapped(send.astype(wire), axis, distance).astype(value.dtype)
+    return value
+
+
+ROWS = 8
+MESH = pl.DeviceIdType.MESH
+
+
+def to_groups(value):
+    return value.reshape(-1, ROWS, value.shape[-1])
+
+
+def add_into(result, result_start, target, start, source, source_start, count):
+    step = 4
+    while count % step:
+        step //= 2
+
+    def one(index, carry):
+        shift = index * step
+        result[pl.ds(result_start + shift, step)] = (
+            target[pl.ds(start + shift, step)] + source[pl.ds(source_start + shift, step)]
+        )
+        return carry
+
+    lax.fori_loop(0, count // step, one, 0)
+
+
+def bit_of(index, bit):
+    return lax.rem(lax.div(index, 2**bit), 2)
+
+
+def partner_of(index, bit):
+    return index + (1 - 2 * bit_of(index, bit)) * 2**bit
+
+
+def stream_plan(total, devices):
+    bits = bit_count(devices)
+    units = -(-total // devices)
+    if bits >= 3:
+        rest = tuple(range(2, bits))
+        orders = [(0, 1) + rest, rest + (0, 1), (1, 0) + rest]
+        weights = [5, 3, 5]
+    else:
+        orders = [tuple(range(bits))]
+        weights = [1]
+    orders, weights = orders * 2, weights * 2
+    shares = [units * weight // sum(weights) for weight in weights]
+    for index in range(units - sum(shares)):
+        shares[index % len(shares)] += 1
+    plan, begin = [], 0
+    for order, share in zip(orders, shares):
+        if share:
+            plan.append((order, begin, share * devices))
+            begin += share * devices
+    return plan, begin
+
+
+def reduce_kernel(
+    plan, dp_bits, tensor_bits, groups, units, qkv_ref, out_ref, gain_ref, mlp_ref,
+    qkv_to, out_to, gain_to, mlp_to, acc, work, got_tensor, got, full,
+    send_sem, recv_sem, tensor_send, tensor_recv, load_sem, mlp_sem,
+):
+    me = lax.axis_index("dp")
+    slot = lax.axis_index("tensor")
+    tensor = 2**tensor_bits
+    width = acc.shape[-1]
+    shared = 4 * groups + 1
+
+    load_mlp = pltpu.make_async_copy(mlp_ref, acc.at[pl.ds(0, units)], mlp_sem.at[0])
+    load_mlp.start()
+    loads = []
+    for part in range(tensor):
+        rows = pl.ds(part * groups, groups)
+        pairs = [
+            (qkv_ref.at[rows, :, pl.ds(block * width, width)], block * groups, groups)
+            for block in range(3)
+        ]
+        pairs.append((out_ref.at[rows], 3 * groups, groups))
+        pairs.append((gain_ref.at[pl.ds(part, 1)], 4 * groups, 1))
+        for source, place, count in pairs:
+            copy = pltpu.make_async_copy(
+                source, work.at[pl.ds(part * shared + place, count)], load_sem.at[len(loads)]
+            )
+            copy.start()
+            loads.append(copy)
+
+    barrier = pltpu.get_barrier_semaphore()
+    for bit in range(dp_bits):
+        pl.semaphore_signal(
+            barrier, inc=1, device_id=(partner_of(me, bit), slot), device_id_type=MESH
+        )
+    for bit in range(tensor_bits):
+        pl.semaphore_signal(
+            barrier, inc=1, device_id=(me, partner_of(slot, bit)), device_id_type=MESH
+        )
+    load_mlp.wait()
+    pl.semaphore_wait(barrier, dp_bits + tensor_bits)
+
+    starts = [[begin] for _, begin, _ in plan]
+
+    def reduce_copy(stream, stage):
+        order, base, share = plan[stream]
+        bit = order[stage]
+        half = share >> (stage + 1)
+        begin = starts[stream][stage]
+        return pltpu.make_async_remote_copy(
+            src_ref=acc.at[pl.ds(begin + (1 - bit_of(me, bit)) * half, half)],
+            dst_ref=got.at[pl.ds(base + share - (share >> stage), half)],
+            send_sem=send_sem.at[stream, stage],
+            recv_sem=recv_sem.at[stream, stage],
+            device_id=(partner_of(me, bit), slot),
+            device_id_type=MESH,
+        )
+
+    def gather_copy(stream, stage):
+        order, _, share = plan[stream]
+        region = pl.ds(starts[stream][stage + 1], share >> (stage + 1))
+        return pltpu.make_async_remote_copy(
+            src_ref=full.at[region],
+            dst_ref=full.at[region],
+            send_sem=send_sem.at[stream, dp_bits + stage],
+            recv_sem=recv_sem.at[stream, dp_bits + stage],
+            device_id=(partner_of(me, order[stage]), slot),
+            device_id_type=MESH,
+        )
+
+    flying = {}
+    for stream, (_, base, share) in enumerate(plan):
+        if base + share <= units:
+            flying[stream] = reduce_copy(stream, 0)
+            flying[stream].start()
+
+    for copy in loads:
+        copy.wait()
+    start, length, place = 0, shared * tensor, 0
+    for stage, bit in enumerate(reversed(range(tensor_bits))):
+        length //= 2
+        mine = bit_of(slot, bit)
+        copy = pltpu.make_async_remote_copy(
+            src_ref=work.at[pl.ds(start + (1 - mine) * length, length)],
+            dst_ref=got_tensor.at[pl.ds(place, length)],
+            send_sem=tensor_send.at[stage],
+            recv_sem=tensor_recv.at[stage],
+            device_id=(me, partner_of(slot, bit)),
+            device_id_type=MESH,
+        )
+        copy.start()
+        copy.wait()
+        start = start + mine * length
+        if stage + 1 < tensor_bits:
+            add_into(work, start, work, start, got_tensor, place, length)
+        else:
+            add_into(acc, units, work, start, got_tensor, place, length)
+        place += length
+    for stream in range(len(plan)):
+        if stream not in flying:
+            flying[stream] = reduce_copy(stream, 0)
+            flying[stream].start()
+
+    for stage in range(dp_bits):
+        for stream, (order, base, share) in enumerate(plan):
+            flying[stream].wait()
+            half = share >> (stage + 1)
+            begin = starts[stream][stage] + bit_of(me, order[stage]) * half
+            starts[stream].append(begin)
+            last = stage + 1 == dp_bits
+            add_into(
+                full if last else acc, begin, acc, begin,
+                got, base + share - (share >> stage), half,
+            )
+            copy = gather_copy(stream, stage) if last else reduce_copy(stream, stage + 1)
+            copy.start()
+            flying[stream] = copy
+    for stage in reversed(range(dp_bits)):
+        for stream in range(len(plan)):
+            flying[stream].wait()
+            if stage:
+                copy = gather_copy(stream, stage - 1)
+                copy.start()
+                flying[stream] = copy
+    pairs = [(mlp_to, 0, units)]
+    for block in range(3):
+        target = qkv_to.at[:, :, pl.ds(block * width, width)]
+        pairs.append((target, units + block * groups, groups))
+    pairs.append((out_to, units + 3 * groups, groups))
+    pairs.append((gain_to, units + 4 * groups, 1))
+    stores = [
+        pltpu.make_async_copy(full.at[pl.ds(place, count)], target, load_sem.at[index])
+        for index, (target, place, count) in enumerate(pairs)
+    ]
+    for copy in stores:
+        copy.start()
+    for copy in stores:
+        copy.wait()
+
+
+def reduce_gradients(qkv, out, gain, mlp):
+    dp_bits = bit_count(lax.axis_size("dp"))
+    tensor = lax.axis_size("tensor")
+    tensor_bits = bit_count(tensor)
+    groups, units, width = out.shape[0] // tensor, mlp.shape[0], out.shape[-1]
+    shared = 4 * groups + 1
+    plan, total = stream_plan(units + shared, 2**dp_bits)
+    bf16 = jnp.bfloat16
+    dma = pltpu.SemaphoreType.DMA
+    filler = total - units - shared
+
+    def kernel(*refs):
+        if filler:
+            refs[8][pl.ds(units + shared, filler)] = jnp.zeros((filler, ROWS, width), bf16)
+        reduce_kernel(plan, dp_bits, tensor_bits, groups, units, *refs)
+
+    def buffer(count):
+        return pltpu.VMEM((count, ROWS, width), bf16)
+
+    return pl.pallas_call(
+        kernel,
+        out_shape=[
+            jax.ShapeDtypeStruct((groups, ROWS, qkv.shape[-1]), bf16),
+            jax.ShapeDtypeStruct((groups, ROWS, width), bf16),
+            jax.ShapeDtypeStruct((1, ROWS, width), bf16),
+            jax.ShapeDtypeStruct((units, ROWS, width), bf16),
+        ],
+        in_specs=[pl.BlockSpec(memory_space=pl.ANY)] * 4,
+        out_specs=[pl.BlockSpec(memory_space=pl.ANY)] * 4,
+        scratch_shapes=[
+            buffer(total),
+            buffer(shared * tensor),
+            buffer(shared * (tensor - 1)),
+            buffer(total),
+            buffer(total),
+            dma((len(plan), 2 * dp_bits)),
+            dma((len(plan), 2 * dp_bits)),
+            dma((tensor_bits,)),
+            dma((tensor_bits,)),
+            dma((max(6, 5 * tensor),)),
+            dma((1,)),
+        ],
+        compiler_params=pltpu.CompilerParams(
+            collective_id=0, has_side_effects=True, vmem_limit_bytes=40 * 2**20
+        ),
+        name="reduce_gradients",
+    )(qkv, out, gain, mlp)
+
+
 def body(layer_in, norm1_gain, qkv_weight, out_weight, norm2_gain, mlp_weight, cotangent):
     f32 = jnp.float32
     bf16 = jnp.bfloat16
@@ -111,10 +380,10 @@
     span = SEQ // rows
     scale = HEAD_DIM ** (-0.5)
     first_norm_gain, second_norm_gain, w_qkv, w_out = (
-        lax.all_gather(norm1_gain, "tensor", axis=0, tiled=True),
-        lax.all_gather(norm2_gain, "tensor", axis=0, tiled=True),
-        lax.all_gather(qkv_weight, "tensor", axis=0, tiled=True),
-        lax.all_gather(out_weight, "tensor", axis=0, tiled=True),
+        gather_rows(norm1_gain, "tensor"),
+        gather_rows(norm2_gain, "tensor"),
+        gather_rows(qkv_weight, "tensor"),
+        gather_rows(out_weight, "tensor"),
     )
     first_norm_gain = first_norm_gain.astype(f32)
     second_norm_gain = second_norm_gain.astype(f32)
@@ -155,29 +424,24 @@
     up_pre = jnp.dot(group, mlp_weight[1], preferred_element_type=f32)
     gel, slope = gelu_parts(gate_pre)
     hidden = (gel * up_pre).astype(bf16)
-    branch = lax.psum_scatter(
-        right_product(hidden, mlp_weight[2]).astype(jnp.bfloat16),
-        "tensor",
-        scatter_dimension=0,
-        tiled=True,
-    ).astype(jnp.float32)
+    branch = scatter_sum(right_product(hidden, mlp_weight[2]), "tensor", bf16)
     layer_out = (attention_mixed + branch).astype(bf16)
     grad_group = lax.all_gather(cotangent, "tensor", axis=0, tiled=True)
     grad_hidden = jnp.dot(grad_group, mlp_weight[2], preferred_element_type=f32)
     grad_gate = (grad_hidden * up_pre * slope).astype(bf16)
     grad_up = (grad_hidden * gel).astype(bf16)
-    grad_mlp = jnp.stack(
+    mlp_share = jnp.concatenate(
         [
-            left_product(group, grad_gate),
-            left_product(group, grad_up),
-            left_product(grad_group, hidden),
-        ]
-    )
-    gradient_hidden_second = lax.psum_scatter(
+            left_product(grad_gate, group).astype(bf16),
+            left_product(grad_up, group).astype(bf16),
+            left_product(hidden, grad_group).astype(bf16),
+        ],
+        0,
+    )
+    gradient_hidden_second = scatter_sum(
         right_product(grad_gate, mlp_weight[0]) + right_product(grad_up, mlp_weight[1]),
         "tensor",
-        scatter_dimension=0,
-        tiled=True,
+        bf16,
     )
     second_norm_backward, gradient_gain_second = layer_norm_backward(
         gradient_hidden_second, standardized_second, inverse_deviation_second, second_norm_gain
@@ -209,28 +473,25 @@
         gradient_hidden_first, standardized_first, inverse_deviation_first, first_norm_gain
     )
     input_grad = grad_mixed + first_norm_backward
-    shares = (
-        lax.psum_scatter(
-            grad_wqkv.astype(jnp.bfloat16), "tensor", scatter_dimension=0, tiled=True
-        ).astype(jnp.float32),
-        lax.psum_scatter(
-            grad_wout.astype(jnp.bfloat16), "tensor", scatter_dimension=0, tiled=True
-        ).astype(jnp.float32),
-        lax.psum_scatter(
-            gradient_gain_first.astype(jnp.bfloat16), "tensor", scatter_dimension=0, tiled=True
-        ).astype(jnp.float32),
-        lax.psum_scatter(
-            gradient_gain_second.astype(jnp.bfloat16), "tensor", scatter_dimension=0, tiled=True
-        ).astype(jnp.float32),
-    )
-    totals = (
-        lax.psum(shares[0].astype(jnp.bfloat16), "dp").astype(jnp.float32),
-        lax.psum(shares[1].astype(jnp.bfloat16), "dp").astype(jnp.float32),
-        lax.psum(shares[2].astype(jnp.bfloat16), "dp").astype(jnp.float32),
-        lax.psum(shares[3].astype(jnp.bfloat16), "dp").astype(jnp.float32),
-        lax.psum(grad_mlp.astype(jnp.bfloat16), "dp").astype(jnp.float32),
-    )
-    return (layer_out, input_grad, totals[2], totals[0], totals[1], totals[3], totals[4])
+    tensor = lax.axis_size("tensor")
+    own = width // tensor
+    units = mlp_weight.shape[2]
+    gains = jnp.stack([gradient_gain_first, gradient_gain_second]).astype(bf16)
+    gains = gains.reshape(2, tensor, own).transpose(1, 0, 2)
+    gains = jnp.pad(gains, ((0, 0), (0, ROWS - 2), (0, width - own)))
+    qkv_total, out_total, gain_total, mlp_total = reduce_gradients(
+        to_groups(grad_wqkv.astype(bf16)), to_groups(grad_wout.astype(bf16)), gains,
+        to_groups(mlp_share),
+    )
+    return (
+        layer_out,
+        input_grad,
+        gain_total[0, 0, :own].astype(f32),
+        qkv_total.reshape(own, 3 * width).astype(f32),
+        out_total.reshape(own, width).astype(f32),
+        gain_total[0, 1, :own].astype(f32),
+        mlp_total.reshape(3, units, width).astype(f32).transpose(0, 2, 1),
+    )
 
 
 def solution(mesh):

time: 341 us -> 215 us (0.63)
  waiting for transfers between devices: 171 us -> 0.03 us
  Pallas kernels: 0 us -> 108 us
  blocking collectives: 55.7 us -> 5.32 us
  between operations: 15.6 us -> 1.31 us
  other arithmetic: 23.5 us -> 27.4 us
    psum x1 -> x0, waiting for transfers between devices: 141 us -> none  [body(): lax.psum(shares[0].astype(jnp.bfloat16), 'dp').astype(jnp.float32)]
    pallas_call x0 -> x1, Pallas kernels: none -> 108 us  [reduce_gradients(): pl.pallas_call(kernel, out_shape=[jax.ShapeDtypeStruct((groups, ROWS, qkv...]
    psum x1 -> x0, blocking collectives: 44.4 us -> none  [body(): lax.psum(shares[2].astype(jnp.bfloat16), 'dp').astype(jnp.float32)]
    reduce_scatter x4 -> x0, waiting for transfers between devices: 18.1 us -> none  [the longest x1 9.36 us: body(): lax.psum_scatter(right_product(hidden, mlp_weight[2]).astype(jnp.bfloat16...]
    all_gather x2 -> x0, waiting for transfers between devices: 11.1 us -> none  [the longest x1 11.1 us: body(): lax.all_gather(qkv_weight, 'tensor', axis=0, tiled=True)]
    convert_element_type x6 -> x5, other arithmetic: 9.56 us -> 5.42 us  [the longest x1 2.02 us: body(): qkv_total.reshape(own, 3 * width).astype(f32)]
    all_gather x2 -> x0, blocking collectives: 3.81 us -> none  [the longest x1 1.98 us: body(): lax.all_gather(norm1_gain, 'tensor', axis=0, tiled=True)]
    unnamed x93 -> x76, local copies, waits for them, and re-layouts: 6.46 us -> 8.11 us
  transfers between devices with their start and end apart: 11 -> 10, of which waited for: 4 -> 0; matrix products, arithmetic and copies ran while one was open for 17% -> 20% of each run, Pallas kernels for 0% -> 0%
where the time goes in v1:
time: 215 us; the launch traced here: 214 us
  Pallas kernels  108 us (50%)
  matrix products  58.6 us (27%)
  other arithmetic  27.4 us (13%)
  local copies, waits for them, and re-layouts  10.5 us (5%)
  blocking collectives  5.32 us (2%)
  starting transfers between devices  2.74 us (1%)
    pallas_call x1, Pallas kernels, reduce_gradients(): pl.pallas_call(kernel, out_shape=[jax.ShapeDtypeStruct((groups, ROWS, qkv...  108 us
    unnamed x76, local copies, waits for them, and re-layouts  8.11 us
    reduce_sum x1, matrix products, body(): total = jnp.log(jnp.sum(jnp.exp(scores), -1))  7.85 us
    dot_general x1, matrix products, body(): jnp.einsum('hqk,qhd->khd', probs_b, grad_att, preferred_element_type=f32)  7.84 us
    dot_general x1, matrix products, body(): jnp.einsum('hqk,khd->qhd', probs_b, values, preferred_element_type=f32)  7.04 us
    dot_general x5, matrix products, left_product(): lax.dot_general(left, right, (((0,), (0,)), ((), ())), preferred_element_...  6.46 us
    dot_general x5, matrix products, right_product(): lax.dot_general(left, weight, (((1,), (1,)), ((), ())), preferred_element...  6.36 us
    dot_general x1, matrix products, body(): jnp.einsum('qhd,khd->hqk', query, keys, preferred_element_type=f32) * scale  4.92 us
  transfers between devices with their start and end apart: 10, of which 0 were waited for; matrix products, arithmetic and copies ran while one was open for 20% of the time, Pallas kernels for 0%

profile of v1, /device:TPU:0, one launch (start us, length us, event | category | flops | bytes accessed | tf_op | source)
XLA Modules:
  0.0 213.8 jit_solution(11962709777526168419)
XLA Ops:
  0.6 0.6 collective-permute-start.1
  1.3 0.4 collective-permute-start.4
  1.8 1.1 convert_reduce_fusion
  2.9 1.2 fusion.57
  4.2 0.8 multiply_cosine_fusion
  5.0 2.6 %all_gather.7 = bf16[512,768]{1,0:T(8,128)(2,1)S(1)} all-gather(bf16[256,768]{1,0:T(8,128)(2,1)} %param.13), channel_id=1, replica_groups=mesh['dp'=16,'tensor'=2] {'tensor'}, dimensions={0}, use_global_device_ids=true | all-gather | bytes 1179648 | tf_op jit(solution)/shard_map/all_gather | solution.py:429
  7.6 0.8 fusion.73
  8.4 1.2 copy-done.35
  9.6 3.4 %fusion.69 = f32[256,2304]{1,0:T(8,128)S(1)} fusion(bf16[384,2304]{1,0:T(8,128)(2,1)} %param.9, bf16[384,2304]{1,0:T(8,128)(2,1)S(1)} %collective-permute-done.1, pred[]{:T(512)S(6)} %eq.23, bf16[256,768]{1,0:T(8,128)(2,1)} %param.7, f32[768]{0:T(1024)S(1)} %fusion.73, f32[256]{0:T(256)S(1)} %add_rsqrt_fusion.1, f32[256]{0:T(256)S(1)} %broadcast_multiply_fusion.5), kind=kOutput, calls=%fused_computation.102 | convolution fusion | flops 922877952 | bytes 6296577 | tf_op jit(solution)/shard_map/dot_general | solution.py:397
  13.2 0.3 copy.27
  13.4 0.9 multiply_subtract_fusion
  14.4 0.4 collective-permute-start.3
  15.0 2.8 %fusion.40 = f32[512,576]{0,1:T(8,128)} fusion(bf16[512,768]{1,0:T(8,128)(2,1)S(1)} %all_gather.7, bf16[3,768,576]{1,2,0:T(8,128)(2,1)} %param.12), kind=kOutput, calls=%fused_computation.51 | convolution fusion | flops 452984832 | bytes 2850816 | tf_op jit(solution)/shard_map/dot_general | solution.py:430
  17.8 0.7 fusion.74
  18.5 0.3 copy.26
  19.1 1.3 copy.24
  20.5 4.9 %fusion.72 = f32[12,256,512]{2,1,0:T(8,128)} fusion(bf16[256,12,32]{0,2,1:T(8,128)(2,1)S(1)} %get-tuple-element.36, bf16[256,12,32]{0,2,1:T(8,128)(2,1)S(1)} %get-tuple-element.35, bf16[256,12,64]{0,2,1:T(8,128)(2,1)S(1)} %maximum_convert_fusion, bf16[256,12,64]{0,2,1:T(8,128)(2,1)} %bitcast.7, pred[]{:T(512)S(6)} %eq.22), kind=kOutput, calls=%fused_computation.117 | convolution fusion | flops 205651968 | bytes 7471105 | tf_op jit(solution)/shard_map/qhd,khd->hqk/dot_general | solution.py:408
  25.4 7.0 %fusion.17 = bf16[12,64,256]{2,1,0:T(8,128)(2,1)S(1)} fusion(f32[12,256,512]{2,1,0:T(8,128)} %fusion.72, bf16[256,12,64]{0,2,1:T(8,128)(2,1)S(1)} %bitcast.99, bf16[256,12,64]{0,2,1:T(8,128)(2,1)S(1)} %bitcast.101, pred[]{:T(512)S(6)} %eq.22), kind=kOutput, calls=%fused_computation.30 | convolution fusion | flops 211357184 | bytes 7471105 | tf_op jit(solution)/shard_map/hqk,khd->qhd/dot_general | solution.py:412
  32.5 2.3 %fusion.97 = (f32[256]{0:T(256)S(1)}, f32[256,768]{1,0:T(8,128)S(1)}) fusion(bf16[256,768]{0,1:T(8,128)(2,1)S(1)} %bitcast.96, bf16[384,768]{1,0:T(8,128)(2,1)} %param.10, bf16[384,768]{1,0:T(8,128)(2,1)} %collective-permute-done.4, pred[]{:T(512)S(6)} %eq.23, bf16[256,768]{1,0:T(8,128)(2,1)S(1)} %copy-done.9), kind=kOutput, calls=%fused_computation.153 | convolution fusion | flops 307887872 | bytes 2753537 | tf_op jit(solution)/shard_map/dot_general | solution.py:416
  34.9 0.2 multiply_reduce_fusion.2
  35.1 0.2 multiply_convert_fusion.3
  35.3 2.7 %all_gather.6 = bf16[512,768]{1,0:T(8,128)(2,1)S(1)} all-gather(bf16[256,768]{1,0:T(8,128)(2,1)S(1)} %multiply_convert_fusion.3), channel_id=1, replica_groups=mesh['dp'=16,'tensor'=2] {'tensor'}, dimensions={0}, use_global_device_ids=true | all-gather | bytes 1179648 | tf_op jit(solution)/shard_map/all_gather | solution.py:422
  38.0 0.7 fusion.45
  38.7 1.2 multiply_convert_fusion.1
  39.9 0.8 fusion.42
  40.7 0.6 convolution_convert_fusion.2
  41.3 0.8 fusion.47
  42.1 0.6 convolution_convert_fusion.4
  42.8 0.6 convolution_convert_fusion.3
  43.4 0.8 convolution_add_fusion
  44.3 0.9 select_convert_fusion.2
  45.1 0.4 collective-permute-start.7
  45.5 0.8 select_convert_fusion.3
  46.5 0.2 maximum_bitcast_fusion.refs_3_
  46.7 7.8 %fusion.1 = f32[12,256,512]{2,1,0:T(8,128)} fusion(bf16[256,12,32]{0,2,1:T(8,128)(2,1)} %copy-done.17, bf16[256,12,32]{0,2,1:T(8,128)(2,1)} %copy-done.15, bf16[256,12,64]{0,2,1:T(8,128)(2,1)} %copy-done.21, bf16[256,12,64]{0,2,1:T(8,128)(2,1)} %bitcast.7, pred[]{:T(512)S(6)} %eq.22), kind=kOutput, calls=%fused_computation.2 | convolution fusion | flops 416026112 | bytes 7471105 | tf_op jit(solution)/shard_map/reduce_sum | solution.py:409
  54.5 2.1 multiply_reduce_fusion
  56.6 2.2 %multiply_add_fusion = (f32[256,768]{1,0:T(8,128)S(1)}, bf16[256,768]{1,0:T(8,128)(2,1)}) fusion(bf16[256,768]{1,0:T(8,128)(2,1)S(1)} %copy-done.26, f32[256,768]{1,0:T(8,128)S(1)} %get-tuple-element.23, f32[256,768]{1,0:T(8,128)S(1)} %get-tuple-element.44, f32[256]{0:T(256)S(1)} %broadcast_multiply_fusion.2, f32[256]{0:T(256)S(1)} %broadcast_multiply_fusion.3, ...), kind=kLoop, calls=%fused_computation.81 | loop fusion | flops 2752512 | bytes 5118977 | tf_op jit(solution)/shard_map/add | solution.py:449
  58.8 0.9 copy-done.4
  59.7 1.8 convolution_convert_fusion.5
  61.7 7.8 %fusion.12 = f32[512,12,64]{0,2,1:T(8,128)} fusion(bf16[256,12,64]{0,2,1:T(8,128)(2,1)S(1)} %bitcast.90, f32[12,256,512]{2,1,0:T(8,128)} %fusion.72), kind=kOutput, calls=%fused_computation.22 | convolution fusion | flops 207621632 | bytes 8257536 | tf_op jit(solution)/shard_map/hqk,qhd->khd/dot_general | solution.py:463
  69.5 2.7 %slice_select_fusion = f32[256,12,64]{0,2,1:T(8,128)} fusion(f32[512,12,64]{0,2,1:T(8,128)} %fusion.12, pred[]{:T(512)S(6)} %eq.22), kind=kLoop, calls=%fused_computation.95 | loop fusion | flops 196608 | bytes 2359297 | tf_op jit(solution)/shard_map/jit(_where)/select_n | solution.py:100
  72.4 3.6 %multiply_convert_fusion = bf16[12,256,512]{2,1,0:T(8,128)(2,1)S(1)} fusion(f32[12,256,512]{2,1,0:T(8,128)} %fusion.1, f32[12,256]{1,0:T(8,128)S(1)} %fusion.59, bf16[256,12,64]{0,2,1:T(8,128)(2,1)S(1)} %bitcast.92, bf16[256,12,64]{0,2,1:T(8,128)(2,1)S(1)} %bitcast.100, bf16[256,12,64]{0,2,1:T(8,128)(2,1)S(1)} %bitcast.102, pred[]{:T(512)S(6)} %eq.22), kind=kOutput, calls=%fused_computation.3 | convolution fusion | flops 209584128 | bytes 10629121 | tf_op jit(solution)/shard_map/qhd,khd->hqk/dot_general | solution.py:456
  76.0 0.7 multiply_bitcast_fusion
  76.7 1.0 copy-done.2
  77.6 0.9 copy-done.6
  78.5 1.0 select_convert_fusion
  79.6 1.0 slice_select_fusion.1
  80.6 0.4 collective-permute-start.8
  80.9 1.5 fusion.15.refs_1_
  82.6 3.5 %fusion.16 = f32[256,12,64]{0,2,1:T(8,128)S(1)} fusion(bf16[12,256,512]{2,1,0:T(8,128)(2,1)} %copy-done.2, bf16[256,12,64]{0,2,1:T(8,128)(2,1)} %copy-done.21, bf16[256,12,64]{0,2,1:T(8,128)(2,1)} %bitcast.7, pred[]{:T(512)S(6)} %eq.22), kind=kOutput, calls=%fused_computation.28 | convolution fusion | flops 205062144 | bytes 4718593 | tf_op jit(solution)/shard_map/hqk,khd->qhd/dot_general | solution.py:461
  86.1 1.1 bitcast_add_fusion.1
  87.3 0.3 add_convert_fusion.2
  87.7 0.7 copy-done.12
  88.4 1.1 fusion.58
  89.6 3.1 %fusion.4.refs_0_ = bf16[96,8,2304]{2,1,0:T(8,128)(2,1)} fusion(bf16[256,768]{0,1:T(8,128)(2,1)S(1)} %fusion.58, bf16[256,768]{0,1:T(8,128)(2,1)S(1)} %bitcast.103, bf16[256,768]{0,1:T(8,128)(2,1)S(1)} %bitcast.105, bf16[256,768]{1,0:T(8,128)(2,1)S(1)} %copy-done.10, f32[768]{0:T(1024)S(1)} %fusion.73, f32[256]{0:T(256)S(1)} %add_rsqrt_fusion.1, ...), kind=kOutput, calls=%fused_computation.9 | convolution fusion | flops 912261120 | bytes 5116928 | tf_op jit(solution)/shard_map/dot_general | solution.py:72
  92.7 2.1 fusion.56
  94.9 1.3 copy-done
  96.1 2.0 copy-done.1
  98.1 107.9 %reduce_gradients.1 = (bf16[48,8,2304]{2,1,0:T(8,128)(2,1)S(1)}, bf16[48,8,768]{2,1,0:T(8,128)(2,1)S(1)}, bf16[1,8,768]{2,1,0:T(8,128)(2,1)S(1)}, bf16[216,8,768]{2,1,0:T(8,128)(2,1)S(1)}) custom-call(bf16[96,8,2304]{2,1,0:T(8,128)(2,1)S(1)} %copy-done.1, bf16[96,8,768]{2,1,0:T(8,128)(2,1)S(1)} %copy-done, bf16[2,8,768]{2,1,0:T(8,128)(2,1)S(1)} %pad.4.refs_2_, ...), custom_call_target="tpu_custom_call" | custom-call | tf_op jit(solution)/shard_map/reduce_gradients/pallas_call | solution.py:345
  206.1 0.6 convert_reduce_fusion.1
  206.7 2.0 bitcast_convert_fusion
  208.7 1.1 bitcast_convert_fusion.1
  209.8 2.8 %convert_bitcast_fusion = f32[3,768,576]{1,2,0:T(8,128)} fusion(bf16[3,576,768]{2,1,0:T(8,128)(2,1)S(1)} %bitcast.89), kind=kLoop, calls=%fused_computation.7 | loop fusion | flops 1327104 | bytes 7962624 | tf_op jit(solution)/shard_map/transpose | solution.py:493
  212.6 1.2 fusion.55
  (107 shorter events, 1.7 us)
Async XLA Ops:
  0.6 7.8 %collective-permute-start.1 = (bf16[384,2304]{1,0:T(8,128)(2,1)}, bf16[384,2304]{1,0:T(8,128)(2,1)S(1)}, u32[]{:S(2)}, u32[]{:S(2)}) collective-permute-start(bf16[384,2304]{1,0:T(8,128)(2,1)} %param.9), channel_id=1, source_target_pairs={{0,1},{1,0},{2,3},{3,2},{4,5},{5,4},{6,7},{7,6},{8,9},{9,8},{10,11... | collective-permute-start | bytes 5308424 | tf_op jit(solution)/shard_map/ppermute | solution.py:20
  1.2 6.5 %collective-permute-start = (bf16[384]{0:T(512)(128)(2,1)}, bf16[384]{0:T(512)(128)(2,1)S(1)}, u32[]{:S(2)}, u32[]{:S(2)}) collective-permute-start(bf16[384]{0:T(512)(128)(2,1)} %param.8), channel_id=1, source_target_pairs={{0,1},{1,0},{2,3},{3,2},{4,5},{5,4},{6,7},{7,6},{8,9},{9,8},{10,11... | collective-permute-start | bytes 2312 | tf_op jit(solution)/shard_map/ppermute | solution.py:20
  1.3 31.2 %collective-permute-start.4 = (bf16[384,768]{1,0:T(8,128)(2,1)}, bf16[384,768]{1,0:T(8,128)(2,1)}, u32[]{:S(2)}, u32[]{:S(2)}) collective-permute-start(bf16[384,768]{1,0:T(8,128)(2,1)} %param.10), channel_id=1, source_target_pairs={{0,1},{1,0},{2,3},{3,2},{4,5},{5,4},{6,7},{7,6},{8,9},{9,8},{10,11... | collective-permute-start | bytes 1769480 | tf_op jit(solution)/shard_map/ppermute | solution.py:20
  1.7 16.1 %collective-permute-start.5 = (bf16[384]{0:T(512)(128)(2,1)}, bf16[384]{0:T(512)(128)(2,1)}, u32[]{:S(2)}, u32[]{:S(2)}) collective-permute-start(bf16[384]{0:T(512)(128)(2,1)} %param.11), channel_id=1, source_target_pairs={{0,1},{1,0},{2,3},{3,2},{4,5},{5,4},{6,7},{7,6},{8,9},{9,8},{10,11... | collective-permute-start | bytes 2312 | tf_op jit(solution)/shard_map/ppermute | solution.py:20
  8.4 1.2 copy-start.35
  14.3 3.5 %copy-start.33 = (bf16[384]{0:T(512)(128)(2,1)S(1)}, bf16[384]{0:T(512)(128)(2,1)}, u32[]{:S(2)}) copy-start(bf16[384]{0:T(512)(128)(2,1)} %param.11) | copy-start | bytes 2308
  14.4 6.1 %copy-start.21 = (bf16[256,12,64]{0,2,1:T(8,128)(2,1)}, bf16[256,12,64]{0,2,1:T(8,128)(2,1)S(1)}, u32[]{:S(2)}) copy-start(bf16[256,12,64]{0,2,1:T(8,128)(2,1)S(1)} %maximum_convert_fusion) | copy-start | bytes 1179652
  14.4 4.4 %copy-start.29 = (f32[256,32]{0,1:T(8,128)S(1)}, f32[256,32]{0,1:T(8,128)}, u32[]{:S(2)}) copy-start(f32[256,32]{0,1:T(8,128)} %get-tuple-element.41) | copy-start | bytes 98308
  14.4 4.4 %copy-start.31 = (f32[256,32]{0,1:T(8,128)S(1)}, f32[256,32]{0,1:T(8,128)}, u32[]{:S(2)}) copy-start(f32[256,32]{0,1:T(8,128)} %get-tuple-element.42) | copy-start | bytes 98308
  14.4 6.1 %collective-permute-start.3 = (bf16[256,768]{0,1:T(8,128)(2,1)S(1)}, bf16[256,768]{0,1:T(8,128)(2,1)}, u32[]{:S(2)}, u32[]{:S(2)}) collective-permute-start(bf16[256,768]{0,1:T(8,128)(2,1)S(1)} %bitcast.98), channel_id=1, source_target_pairs={{0,1},{1,0},{2,3},{3,2},{4,5},{5,4},{6,7},{7,6},{8,9},{9,8},{10,11... | collective-permute-start | bytes 1179656 | tf_op jit(solution)/shard_map/ppermute | solution.py:20
  14.8 4.3 %collective-permute-start.2 = (bf16[256,768]{1,0:T(8,128)(2,1)S(1)}, bf16[256,768]{1,0:T(8,128)(2,1)}, u32[]{:S(2)}, u32[]{:S(2)}) collective-permute-start(bf16[256,768]{1,0:T(8,128)(2,1)S(1)} %slice.190), channel_id=1, source_target_pairs={{0,1},{1,0},{2,3},{3,2},{4,5},{5,4},{6,7},{7,6},{8,9},{9,8},{10,11... | collective-permute-start | bytes 1179656 | tf_op jit(solution)/shard_map/ppermute | solution.py:20
  18.9 6.5 %copy-start.15 = (bf16[256,12,32]{0,2,1:T(8,128)(2,1)}, bf16[256,12,32]{0,2,1:T(8,128)(2,1)S(1)}, u32[]{:S(2)}) copy-start(bf16[256,12,32]{0,2,1:T(8,128)(2,1)S(1)} %get-tuple-element.35) | copy-start | bytes 589828
  18.9 6.5 %copy-start.17 = (bf16[256,12,32]{0,2,1:T(8,128)(2,1)}, bf16[256,12,32]{0,2,1:T(8,128)(2,1)S(1)}, u32[]{:S(2)}) copy-start(bf16[256,12,32]{0,2,1:T(8,128)(2,1)S(1)} %get-tuple-element.36) | copy-start | bytes 589828
  19.1 6.3 %copy-start.22 = (bf16[256,768]{0,1:T(8,128)(2,1)}, bf16[256,768]{0,1:T(8,128)(2,1)S(1)}, u32[]{:S(2)}) copy-start(bf16[256,768]{0,1:T(8,128)(2,1)S(1)} %copy.25) | copy-start | bytes 1179652
  20.4 5.0 %copy-start.24 = (bf16[256,768]{0,1:T(8,128)(2,1)}, bf16[256,768]{0,1:T(8,128)(2,1)S(1)}, u32[]{:S(2)}) copy-start(bf16[256,768]{0,1:T(8,128)(2,1)S(1)} %copy.24) | copy-start | bytes 1179652
  25.4 7.1 %copy-start.9 = (bf16[256,768]{1,0:T(8,128)(2,1)S(1)}, bf16[256,768]{1,0:T(8,128)(2,1)}, u32[]{:S(2)}) copy-start(bf16[256,768]{1,0:T(8,128)(2,1)} %param.7) | copy-start | bytes 1179652
  32.5 2.4 %copy-start.19 = (bf16[12,64,256]{2,1,0:T(8,128)(2,1)}, bf16[12,64,256]{2,1,0:T(8,128)(2,1)S(1)}, u32[]{:S(2)}) copy-start(bf16[12,64,256]{2,1,0:T(8,128)(2,1)S(1)} %fusion.17) | copy-start | bytes 1179652
  34.9 3.1 %copy-start.14 = (bf16[3,768,576]{1,2,0:T(8,128)(2,1)S(1)}, bf16[3,768,576]{1,2,0:T(8,128)(2,1)}, u32[]{:S(2)}) copy-start(bf16[3,768,576]{1,2,0:T(8,128)(2,1)} %param.12) | copy-start | bytes 7962628
  35.1 3.5 %copy-start.27 = (f32[512,576]{0,1:T(8,128)S(1)}, f32[512,576]{0,1:T(8,128)}, u32[]{:S(2)}) copy-start(f32[512,576]{0,1:T(8,128)} %fusion.40) | copy-start | bytes 3538948
  40.7 4.8 %copy-start.7 = (f32[512,768]{1,0:T(8,128)}, f32[512,768]{1,0:T(8,128)S(1)}, u32[]{:S(2)}) copy-start(f32[512,768]{1,0:T(8,128)S(1)} %fusion.42) | copy-start | bytes 4718596
  44.2 2.1 copy-start.3
  45.1 9.4 %collective-permute-start.7 = (bf16[256,768]{1,0:T(8,128)(2,1)}, bf16[256,768]{1,0:T(8,128)(2,1)}, u32[]{:S(2)}, u32[]{:S(2)}) collective-permute-start(bf16[256,768]{1,0:T(8,128)(2,1)} %select_convert_fusion.2), channel_id=1, source_target_pairs={{0,1},{1,0},{2,3},{3,2},{4,5},{5,4},{6,7},{7,6},{8,9},{9,8},{10,11... | collective-permute-start | bytes 1179656 | tf_op jit(solution)/shard_map/ppermute | solution.py:20
  46.3 10.2 %collective-permute-start.6 = (bf16[256,768]{1,0:T(8,128)(2,1)}, bf16[256,768]{1,0:T(8,128)(2,1)}, u32[]{:S(2)}, u32[]{:S(2)}) collective-permute-start(bf16[256,768]{1,0:T(8,128)(2,1)} %select_convert_fusion.3), channel_id=1, source_target_pairs={{0,1},{1,0},{2,3},{3,2},{4,5},{5,4},{6,7},{7,6},{8,9},{9,8},{10,11... | collective-permute-start | bytes 1179656 | tf_op jit(solution)/shard_map/ppermute | solution.py:20
  54.5 2.1 copy-start.8
  54.5 2.1 copy-start.26
  56.6 3.1 %copy-start.37 = (bf16[384,768]{1,0:T(8,128)(2,1)S(1)}, bf16[384,768]{1,0:T(8,128)(2,1)}, u32[]{:S(2)}) copy-start(bf16[384,768]{1,0:T(8,128)(2,1)} %param.10) | copy-start | bytes 1769476
  58.8 0.9 copy-start.4
  69.5 2.7 %copy-start.20 = (bf16[12,64,256]{2,1,0:T(8,128)(2,1)S(1)}, bf16[12,64,256]{2,1,0:T(8,128)(2,1)}, u32[]{:S(2)}) copy-start(bf16[12,64,256]{2,1,0:T(8,128)(2,1)} %copy-done.19) | copy-start | bytes 1179652
  69.5 2.8 %copy-start.23 = (bf16[256,768]{0,1:T(8,128)(2,1)S(1)}, bf16[256,768]{0,1:T(8,128)(2,1)}, u32[]{:S(2)}) copy-start(bf16[256,768]{0,1:T(8,128)(2,1)} %copy-done.22) | copy-start | bytes 1179652
  69.5 2.8 %copy-start.25 = (bf16[256,768]{0,1:T(8,128)(2,1)S(1)}, bf16[256,768]{0,1:T(8,128)(2,1)}, u32[]{:S(2)}) copy-start(bf16[256,768]{0,1:T(8,128)(2,1)} %copy-done.24) | copy-start | bytes 1179652
  72.4 3.6 %copy-start.16 = (bf16[256,12,32]{0,2,1:T(8,128)(2,1)S(1)}, bf16[256,12,32]{0,2,1:T(8,128)(2,1)}, u32[]{:S(2)}) copy-start(bf16[256,12,32]{0,2,1:T(8,128)(2,1)} %copy-done.15) | copy-start | bytes 589828
  72.4 3.6 %copy-start.18 = (bf16[256,12,32]{0,2,1:T(8,128)(2,1)S(1)}, bf16[256,12,32]{0,2,1:T(8,128)(2,1)}, u32[]{:S(2)}) copy-start(bf16[256,12,32]{0,2,1:T(8,128)(2,1)} %copy-done.17) | copy-start | bytes 589828
  76.0 1.7 copy-start.2
  76.0 2.5 %copy-start.6 = (f32[512,12,64]{0,2,1:T(8,128)S(1)}, f32[512,12,64]{0,2,1:T(8,128)}, u32[]{:S(2)}) copy-start(f32[512,12,64]{0,2,1:T(8,128)} %fusion.12) | copy-start | bytes 4718596
  78.5 2.4 %copy-start.5 = (f32[256,768]{1,0:T(8,128)S(1)}, f32[256,768]{1,0:T(8,128)}, u32[]{:S(2)}) copy-start(f32[256,768]{1,0:T(8,128)} %copy-done.4) | copy-start | bytes 2359300
  80.6 5.6 %collective-permute-start.8 = (bf16[256,768]{0,1:T(8,128)(2,1)}, bf16[256,768]{0,1:T(8,128)(2,1)}, u32[]{:S(2)}, u32[]{:S(2)}) collective-permute-start(bf16[256,768]{0,1:T(8,128)(2,1)} %bitcast.21), channel_id=1, source_target_pairs={{0,1},{1,0},{2,3},{3,2},{4,5},{5,4},{6,7},{7,6},{8,9},{9,8},{10,11... | collective-permute-start | bytes 1179656 | tf_op jit(solution)/shard_map/ppermute | solution.py:20
  82.4 5.2 %collective-permute-start.9 = (bf16[256,768]{0,1:T(8,128)(2,1)}, bf16[256,768]{0,1:T(8,128)(2,1)}, u32[]{:S(2)}, u32[]{:S(2)}) collective-permute-start(bf16[256,768]{0,1:T(8,128)(2,1)} %bitcast.26), channel_id=1, source_target_pairs={{0,1},{1,0},{2,3},{3,2},{4,5},{5,4},{6,7},{7,6},{8,9},{9,8},{10,11... | collective-permute-start | bytes 1179656 | tf_op jit(solution)/shard_map/ppermute | solution.py:20
  82.6 3.5 %copy-start.13 = (f32[256,12,64]{0,2,1:T(8,128)S(1)}, f32[256,12,64]{0,2,1:T(8,128)}, u32[]{:S(2)}) copy-start(f32[256,12,64]{0,2,1:T(8,128)} %slice_select_fusion.1) | copy-start | bytes 2359300
  82.6 4.7 %copy-start.30 = (f32[256,32]{0,1:T(8,128)S(1)}, f32[256,32]{0,1:T(8,128)}, u32[]{:S(2)}) copy-start(f32[256,32]{0,1:T(8,128)} %get-tuple-element.41) | copy-start | bytes 98308
  82.6 4.7 %copy-start.32 = (f32[256,32]{0,1:T(8,128)S(1)}, f32[256,32]{0,1:T(8,128)}, u32[]{:S(2)}) copy-start(f32[256,32]{0,1:T(8,128)} %get-tuple-element.42) | copy-start | bytes 98308
  87.3 1.1 copy-start.12
  87.3 2.3 %copy-start.10 = (bf16[256,768]{1,0:T(8,128)(2,1)S(1)}, bf16[256,768]{1,0:T(8,128)(2,1)}, u32[]{:S(2)}) copy-start(bf16[256,768]{1,0:T(8,128)(2,1)} %param.7) | copy-start | bytes 1179652
  89.6 3.1 %copy-start.34 = (bf16[384,2304]{1,0:T(8,128)(2,1)S(1)}, bf16[384,2304]{1,0:T(8,128)(2,1)}, u32[]{:S(2)}) copy-start(bf16[384,2304]{1,0:T(8,128)(2,1)} %param.9) | copy-start | bytes 5308420
  89.6 3.1 %copy-start.36 = (bf16[384,2304]{1,0:T(8,128)(2,1)S(1)}, bf16[384,2304]{1,0:T(8,128)(2,1)}, u32[]{:S(2)}) copy-start(bf16[384,2304]{1,0:T(8,128)(2,1)} %copy-done.35) | copy-start | bytes 5308420
  94.9 1.3 copy-start
  96.1 2.0 copy-start.1
  209.8 2.8 %copy-start.11 = (bf16[256,768]{1,0:T(8,128)(2,1)S(1)}, bf16[256,768]{1,0:T(8,128)(2,1)}, u32[]{:S(2)}) copy-start(bf16[256,768]{1,0:T(8,128)(2,1)} %param.7) | copy-start | bytes 1179652
  209.8 2.8 %copy-start.28 = (f32[256,768]{1,0:T(8,128)S(1)}, f32[256,768]{1,0:T(8,128)}, u32[]{:S(2)}) copy-start(f32[256,768]{1,0:T(8,128)} %get-tuple-element.45) | copy-start | bytes 2359300

commit v2 on v1

--- a/solution.py
+++ b/solution.py
@@ -162,16 +162,48 @@
     return index + (1 - 2 * bit_of(index, bit)) * 2**bit
 
 
+def link_orders(bits):
+    if bits < 3:
+        return [tuple(range(bits))] * 3
+    rest = tuple(range(2, bits))
+    return [(0, 1) + rest, rest + (0, 1), (1, 0) + rest]
+
+
+def halvings(count, bits):
+    stages = 0
+    while stages < bits and (count >> stages) % 2 == 0:
+        stages += 1
+    return stages
+
+
+def sum_stage(values, stage):
+    index = lax.axis_index("dp")
+    bits = bit_count(lax.axis_size("dp"))
+    if stage >= bits:
+        return values
+    results = []
+    for value, order in zip(values, link_orders(bits)):
+        bit = order[stage]
+        if value.shape[0] % 2 == 0:
+            middle = value.shape[0] // 2
+            upper = (index >> bit) % 2 == 1
+            keep = jnp.where(upper, value[middle:], value[:middle])
+            send = jnp.where(upper, value[:middle], value[middle:])
+        else:
+            keep = send = value
+        results.append(keep + swapped(send, "dp", bit))
+    return results
+
+
+def tied(value, chunks):
+    value, *chunks = lax.optimization_barrier((value, *chunks))
+    return value, chunks
+
+
 def stream_plan(total, devices):
-    bits = bit_count(devices)
     units = -(-total // devices)
-    if bits >= 3:
-        rest = tuple(range(2, bits))
-        orders = [(0, 1) + rest, rest + (0, 1), (1, 0) + rest]
-        weights = [5, 3, 5]
-    else:
-        orders = [tuple(range(bits))]
-        weights = [1]
+    orders = link_orders(bit_count(devices))
+    weights = [5, 3, 5]
     orders, weights = orders * 2, weights * 2
     shares = [units * weight // sum(weights) for weight in weights]
     for index in range(units - sum(shares)):
@@ -186,8 +218,8 @@
 
 def reduce_kernel(
     plan, dp_bits, tensor_bits, groups, units, qkv_ref, out_ref, gain_ref, mlp_ref,
-    qkv_to, out_to, gain_to, mlp_to, acc, work, got_tensor, got, full,
-    send_sem, recv_sem, tensor_send, tensor_recv, load_sem, mlp_sem,
+    qkv_to, out_to, gain_to, mlp_to, acc, work, got_tensor, got, full, whole,
+    send_sem, recv_sem, tensor_send, tensor_recv, load_sem, mlp_sem, piece_send, piece_recv,
 ):
     me = lax.axis_index("dp")
     slot = lax.axis_index("tensor")
@@ -195,8 +227,34 @@
     width = acc.shape[-1]
     shared = 4 * groups + 1
 
-    load_mlp = pltpu.make_async_copy(mlp_ref, acc.at[pl.ds(0, units)], mlp_sem.at[0])
-    load_mlp.start()
+    piece = units // 3
+    stages = halvings(piece, dp_bits)
+    chunk = piece >> stages
+    places, piece_loads = [], []
+    for index, order in enumerate(link_orders(dp_bits)):
+        places.append([index * piece])
+        for stage in range(stages):
+            step = bit_of(me, order[stage]) * (piece >> (stage + 1))
+            places[index].append(places[index][stage] + step)
+        copy = pltpu.make_async_copy(
+            mlp_ref.at[pl.ds(index * chunk, chunk)],
+            whole.at[pl.ds(places[index][stages], chunk)],
+            mlp_sem.at[index],
+        )
+        copy.start()
+        piece_loads.append(copy)
+
+    def piece_copy(index, stage):
+        region = pl.ds(places[index][stage + 1], piece >> (stage + 1))
+        return pltpu.make_async_remote_copy(
+            src_ref=whole.at[region],
+            dst_ref=whole.at[region],
+            send_sem=piece_send.at[index, stage],
+            recv_sem=piece_recv.at[index, stage],
+            device_id=(partner_of(me, link_orders(dp_bits)[index][stage]), slot),
+            device_id_type=MESH,
+        )
+
     loads = []
     for part in range(tensor):
         rows = pl.ds(part * groups, groups)
@@ -222,7 +280,8 @@
         pl.semaphore_signal(
             barrier, inc=1, device_id=(me, partner_of(slot, bit)), device_id_type=MESH
         )
-    load_mlp.wait()
+    for copy in piece_loads:
+        copy.wait()
     pl.semaphore_wait(barrier, dp_bits + tensor_bits)
 
     starts = [[begin] for _, begin, _ in plan]
@@ -253,11 +312,11 @@
             device_id_type=MESH,
         )
 
-    flying = {}
-    for stream, (_, base, share) in enumerate(plan):
-        if base + share <= units:
-            flying[stream] = reduce_copy(stream, 0)
-            flying[stream].start()
+    moving = []
+    if stages:
+        moving = [piece_copy(index, stages - 1) for index in range(3)]
+        for copy in moving:
+            copy.start()
 
     for copy in loads:
         copy.wait()
@@ -279,12 +338,12 @@
         if stage + 1 < tensor_bits:
             add_into(work, start, work, start, got_tensor, place, length)
         else:
-            add_into(acc, units, work, start, got_tensor, place, length)
+            add_into(acc, 0, work, start, got_tensor, place, length)
         place += length
+    flying = []
     for stream in range(len(plan)):
-        if stream not in flying:
-            flying[stream] = reduce_copy(stream, 0)
-            flying[stream].start()
+        flying.append(reduce_copy(stream, 0))
+        flying[stream].start()
 
     for stage in range(dp_bits):
         for stream, (order, base, share) in enumerate(plan):
@@ -300,6 +359,15 @@
             copy = gather_copy(stream, stage) if last else reduce_copy(stream, stage + 1)
             copy.start()
             flying[stream] = copy
+        ahead = stages - 1 - stage
+        if ahead >= 0:
+            for index in range(3):
+                moving[index].wait()
+                if ahead:
+                    moving[index] = piece_copy(index, ahead - 1)
+                    moving[index].start()
+    store_mlp = pltpu.make_async_copy(whole, mlp_to, mlp_sem.at[0])
+    store_mlp.start()
     for stage in reversed(range(dp_bits)):
         for stream in range(len(plan)):
             flying[stream].wait()
@@ -307,12 +375,12 @@
                 copy = gather_copy(stream, stage - 1)
                 copy.start()
                 flying[stream] = copy
-    pairs = [(mlp_to, 0, units)]
+    pairs = []
     for block in range(3):
         target = qkv_to.at[:, :, pl.ds(block * width, width)]
-        pairs.append((target, units + block * groups, groups))
-    pairs.append((out_to, units + 3 * groups, groups))
-    pairs.append((gain_to, units + 4 * groups, 1))
+        pairs.append((target, block * groups, groups))
+    pairs.append((out_to, 3 * groups, groups))
+    pairs.append((gain_to, 4 * groups, 1))
     stores = [
         pltpu.make_async_copy(full.at[pl.ds(place, count)], target, load_sem.at[index])
         for index, (target, place, count) in enumerate(pairs)
@@ -321,22 +389,24 @@
         copy.start()
     for copy in stores:
         copy.wait()
-
-
-def reduce_gradients(qkv, out, gain, mlp):
+    store_mlp.wait()
+
+
+def reduce_gradients(qkv, out, gain, mlp, units):
     dp_bits = bit_count(lax.axis_size("dp"))
     tensor = lax.axis_size("tensor")
     tensor_bits = bit_count(tensor)
-    groups, units, width = out.shape[0] // tensor, mlp.shape[0], out.shape[-1]
+    groups, width = out.shape[0] // tensor, out.shape[-1]
+    stages = max(1, halvings(units // 3, dp_bits))
     shared = 4 * groups + 1
-    plan, total = stream_plan(units + shared, 2**dp_bits)
+    plan, total = stream_plan(shared, 2**dp_bits)
     bf16 = jnp.bfloat16
     dma = pltpu.SemaphoreType.DMA
-    filler = total - units - shared
+    filler = total - shared
 
     def kernel(*refs):
         if filler:
-            refs[8][pl.ds(units + shared, filler)] = jnp.zeros((filler, ROWS, width), bf16)
+            refs[8][pl.ds(shared, filler)] = jnp.zeros((filler, ROWS, width), bf16)
         reduce_kernel(plan, dp_bits, tensor_bits, groups, units, *refs)
 
     def buffer(count):
@@ -358,12 +428,15 @@
             buffer(shared * (tensor - 1)),
             buffer(total),
             buffer(total),
+            buffer(units),
             dma((len(plan), 2 * dp_bits)),
             dma((len(plan), 2 * dp_bits)),
             dma((tensor_bits,)),
             dma((tensor_bits,)),
             dma((max(6, 5 * tensor),)),
-            dma((1,)),
+            dma((3,)),
+            dma((3, stages)),
+            dma((3, stages)),
         ],
         compiler_params=pltpu.CompilerParams(
             collective_id=0, has_side_effects=True, vmem_limit_bytes=40 * 2**20
@@ -406,7 +479,9 @@
     keys = key_all.reshape(SEQ, HEADS, HEAD_DIM)
     values = value_all.reshape(SEQ, HEADS, HEAD_DIM)
     scores = jnp.einsum("qhd,khd->hqk", query, keys, preferred_element_type=f32) * scale
-    total = jnp.log(jnp.sum(jnp.exp(scores), -1))
+    highest = jnp.max(scores, -1)
+    total = highest + jnp.log(jnp.sum(jnp.exp(scores - highest[..., None]), -1))
+    total = lax.optimization_barrier(total)
     probs_b = jnp.exp(scores - total[..., None]).astype(bf16)
     attended = (
         jnp.einsum("hqk,khd->qhd", probs_b, values, preferred_element_type=f32)
@@ -430,14 +505,11 @@
     grad_hidden = jnp.dot(grad_group, mlp_weight[2], preferred_element_type=f32)
     grad_gate = (grad_hidden * up_pre * slope).astype(bf16)
     grad_up = (grad_hidden * gel).astype(bf16)
-    mlp_share = jnp.concatenate(
-        [
-            left_product(grad_gate, group).astype(bf16),
-            left_product(grad_up, group).astype(bf16),
-            left_product(hidden, grad_group).astype(bf16),
-        ],
-        0,
-    )
+    mlp_pieces = [
+        to_groups(left_product(left, right).astype(bf16))
+        for left, right in ((grad_gate, group), (grad_up, group), (hidden, grad_group))
+    ]
+    mlp_chunks = sum_stage(mlp_pieces, 0)
     gradient_hidden_second = scatter_sum(
         right_product(grad_gate, mlp_weight[0]) + right_product(grad_up, mlp_weight[1]),
         "tensor",
@@ -449,7 +521,9 @@
     grad_mixed = dz_f + second_norm_backward
     grad_mixed_b = grad_mixed.astype(bf16)
     grad_wout = left_product(attended, grad_mixed_b)
-    grad_att = right_product(grad_mixed_b, w_out).astype(bf16).reshape(rows, HEADS, HEAD_DIM)
+    grad_att, mlp_chunks = tied(right_product(grad_mixed_b, w_out).astype(bf16), mlp_chunks)
+    grad_att = grad_att.reshape(rows, HEADS, HEAD_DIM)
+    mlp_chunks = sum_stage(mlp_chunks, 1)
     scores = jnp.einsum("qhd,khd->hqk", query, keys, preferred_element_type=f32) * scale
     probs = jnp.exp(scores - total[..., None])
     probs_b = probs.astype(bf16)
@@ -458,6 +532,8 @@
         "qhd,qhd->hq", grad_att.astype(f32), attended.reshape(rows, HEADS, HEAD_DIM).astype(f32)
     )
     grad_scores = (probs * (grad_probs - delta[..., None])).astype(bf16)
+    grad_scores, mlp_chunks = tied(grad_scores, mlp_chunks)
+    mlp_chunks = sum_stage(mlp_chunks, 2)
     grad_query = jnp.einsum("hqk,khd->qhd", grad_scores, keys, preferred_element_type=f32) * scale
     grad_keys = jnp.einsum("hqk,qhd->khd", grad_scores, query, preferred_element_type=f32) * scale
     grad_values = jnp.einsum("hqk,qhd->khd", probs_b, grad_att, preferred_element_type=f32)
@@ -468,6 +544,9 @@
     grad_k = unrotate(key_total.reshape(rows, HEADS, HEAD_DIM), cosine, sine).reshape(rows, width)
     grad_qkv = jnp.concatenate([grad_q, grad_k, value_total], 1).astype(bf16)
     grad_wqkv = left_product(h1, grad_qkv)
+    grad_qkv, mlp_chunks = tied(grad_qkv, mlp_chunks)
+    for stage in range(3, bit_count(lax.axis_size("dp"))):
+        mlp_chunks = sum_stage(mlp_chunks, stage)
     gradient_hidden_first = right_product(grad_qkv, w_qkv)
     first_norm_backward, gradient_gain_first = layer_norm_backward(
         gradient_hidden_first, standardized_first, inverse_deviation_first, first_norm_gain
@@ -481,7 +560,7 @@
     gains = jnp.pad(gains, ((0, 0), (0, ROWS - 2), (0, width - own)))
     qkv_total, out_total, gain_total, mlp_total = reduce_gradients(
         to_groups(grad_wqkv.astype(bf16)), to_groups(grad_wout.astype(bf16)), gains,
-        to_groups(mlp_share),
+        jnp.concatenate(mlp_chunks, 0), 3 * mlp_pieces[0].shape[0],
     )
     return (
         layer_out,

time: 215 us -> 199 us (0.926)
  Pallas kernels: 108 us -> 75.3 us
  starting transfers between devices: 2.74 us -> 19.9 us
  matrix products: 58.6 us -> 43.1 us
  waiting for transfers between devices: 0.03 us -> 10.1 us
  other arithmetic: 27.4 us -> 33.2 us
    pallas_call x1, Pallas kernels: 108 us -> 75.3 us  [reduce_gradients(): pl.pallas_call(kernel, out_shape=[jax.ShapeDtypeStruct((groups, ROWS, qkv...]
    ppermute x10 -> x22, starting transfers between devices: 2.74 us -> 19.9 us  [swapped(): return lax.ppermute(value, axis, pairs)]
    ppermute x10 -> x22, waiting for transfers between devices: 0.03 us -> 10.1 us  [swapped(): return lax.ppermute(value, axis, pairs)]
    add x0 -> x13, other arithmetic: none -> 9.14 us  [the longest x12 9.13 us: sum_stage(): results.append(keep + swapped(send, 'dp', bit))]
    reduce_sum x1 -> x0, matrix products: 7.85 us -> none  [body(): total = jnp.log(jnp.sum(jnp.exp(scores), -1))]
    select_n x0 -> x9, other arithmetic: none -> 4.69 us  [sum_stage(): send = jnp.where(upper, value[:middle], value[middle:])]
    unnamed x76 -> x70, local copies, waits for them, and re-layouts: 8.11 us -> 3.48 us
    dot_general x1, matrix products: 7.84 us -> 4.15 us  [body(): jnp.einsum('hqk,qhd->khd', probs_b, grad_att, preferred_element_type=f32)]
  transfers between devices with their start and end apart: 10 -> 22, of which waited for: 0 -> 6; matrix products, arithmetic and copies ran while one was open for 20% -> 31% of each run, Pallas kernels for 0% -> 0%
where the time goes in v2:
time: 199 us; the launch traced here: 198 us
  Pallas kernels  75.3 us (38%)
  matrix products  43.1 us (22%)
  other arithmetic  33.2 us (17%)
  starting transfers between devices  19.9 us (10%)
  waiting for transfers between devices  10.1 us (5%)
  local copies, waits for them, and re-layouts  9.9 us (5%)
  blocking collectives  5.3 us (3%)
    pallas_call x1, Pallas kernels, reduce_gradients(): pl.pallas_call(kernel, out_shape=[jax.ShapeDtypeStruct((groups, ROWS, qkv...  75.3 us
    ppermute x22, starting transfers between devices, swapped(): return lax.ppermute(value, axis, pairs)  19.9 us
    ppermute x22, waiting for transfers between devices, swapped(): return lax.ppermute(value, axis, pairs)  10.1 us
    add x12, other arithmetic, sum_stage(): results.append(keep + swapped(send, 'dp', bit))  9.13 us
    dot_general x5, matrix products, right_product(): lax.dot_general(left, weight, (((1,), (1,)), ((), ())), preferred_element...  8.53 us
    dot_general x5, matrix products, left_product(): lax.dot_general(left, right, (((0,), (0,)), ((), ())), preferred_element_...  5.43 us
    select_n x9, other arithmetic, sum_stage(): send = jnp.where(upper, value[:middle], value[middle:])  4.69 us
    dot_general x1, matrix products, body(): jnp.einsum('hqk,khd->qhd', probs_b, values, preferred_element_type=f32)  4.42 us
  transfers between devices with their start and end apart: 22, of which 6 were waited for; matrix products, arithmetic and copies ran while one was open for 31% of the time, Pallas kernels for 0%

profile of v2, /device:TPU:0, one launch (start us, length us, event | category | flops | bytes accessed | tf_op | source)
XLA Modules:
  0.0 198.3 jit_solution(8178055138663628020)
XLA Ops:
  1.8 1.1 convert_reduce_fusion
  3.0 1.2 fusion.33
  4.2 0.8 multiply_cosine_fusion
  5.1 2.6 %all_gather.7 = bf16[512,768]{1,0:T(8,128)(2,1)S(1)} all-gather(bf16[256,768]{1,0:T(8,128)(2,1)} %param.13), channel_id=1, replica_groups=mesh['dp'=16,'tensor'=2] {'tensor'}, dimensions={0}, use_global_device_ids=true | all-gather | bytes 1179648 | tf_op jit(solution)/shard_map/all_gather | solution.py:504
  7.7 4.0 %fusion.43 = f32[256,2304]{1,0:T(8,128)S(1)} fusion(bf16[384,2304]{1,0:T(8,128)(2,1)} %param.9, bf16[384,2304]{1,0:T(8,128)(2,1)} %collective-permute-done.1, pred[]{:T(512)S(6)} %eq.49, bf16[256,768]{1,0:T(8,128)(2,1)S(1)} %copy-done.7, f32[768]{0:T(1024)S(1)} %fusion.49, f32[256]{0:T(256)S(1)} %add_rsqrt_fusion.1, f32[256]{0:T(256)S(1)} %broadcast_multiply_fusion.5), kind=kOutput, calls=%fused_computation.93 | convolution fusion | flops 922877952 | bytes 6296577 | tf_op jit(solution)/shard_map/dot_general | solution.py:470
  11.9 1.3 copy-done.12
  13.5 0.9 multiply_subtract_fusion
  14.4 0.8 maximum_convert_fusion
  15.5 2.8 %fusion.16 = f32[512,576]{0,1:T(8,128)} fusion(bf16[512,768]{1,0:T(8,128)(2,1)S(1)} %all_gather.7, bf16[3,768,576]{1,2,0:T(8,128)(2,1)} %param.12), kind=kOutput, calls=%fused_computation.43 | convolution fusion | flops 452984832 | bytes 2850816 | tf_op jit(solution)/shard_map/dot_general | solution.py:505
  18.4 0.8 fusion.50
  19.1 1.2 slice.328
  20.5 0.9 copy.25
  21.9 2.5 %multiply_reduce_fusion = (f32[12,256]{1,0:T(8,128)S(1)}, f32[12,256,512]{2,1,0:T(8,128)S(1)}) fusion(bf16[256,12,64]{0,2,1:T(8,128)(2,1)} %maximum_convert_fusion, bf16[256,12,64]{0,2,1:T(8,128)(2,1)} %bitcast.7, pred[]{:T(512)S(6)} %eq.48, bf16[256,12,32]{0,2,1:T(8,128)(2,1)S(1)} %get-tuple-element.60, bf16[256,12,32]{0,2,1:T(8,128)(2,1)S(1)} %get-tuple-element.59), kind=kOutput, calls=%fused_computation.5 | convolution fusion | flops 208794624 | bytes 7483393 | tf_op jit(solution)/shard_map/qhd,khd->hqk/dot_general | solution.py:481
  24.4 1.6 exponential_reduce_fusion
  26.0 1.0 copy-done.1
  27.1 1.2 copy.24
  28.3 4.4 %convolution_convert_fusion.6 = bf16[12,64,256]{2,1,0:T(8,128)(2,1)S(1)} fusion(f32[12,256,512]{2,1,0:T(8,128)} %copy-done.1, f32[12,256]{1,0:T(8,128)S(1)} %log_add_fusion, bf16[256,12,64]{0,2,1:T(8,128)(2,1)S(1)} %bitcast.113, bf16[256,12,64]{0,2,1:T(8,128)(2,1)S(1)} %bitcast.115, pred[]{:T(512)S(6)} %eq.48), kind=kOutput, calls=%fused_computation.23 | convolution fusion | flops 209780736 | bytes 7483393 | tf_op jit(solution)/shard_map/hqk,khd->qhd/dot_general | solution.py:487
  32.8 2.0 %fusion.65 = (f32[256]{0:T(256)S(1)}, f32[256,768]{1,0:T(8,128)S(1)}) fusion(bf16[256,768]{0,1:T(8,128)(2,1)S(1)} %bitcast.107, bf16[384,768]{1,0:T(8,128)(2,1)S(1)} %copy-done.34, bf16[384,768]{1,0:T(8,128)(2,1)} %collective-permute-done.4, pred[]{:T(512)S(6)} %eq.49, bf16[256,768]{1,0:T(8,128)(2,1)S(1)} %copy-done.7), kind=kOutput, calls=%fused_computation.160 | convolution fusion | flops 307887872 | bytes 2753537 | tf_op jit(solution)/shard_map/dot_general | solution.py:491
  35.2 2.7 %all_gather.6 = bf16[512,768]{1,0:T(8,128)(2,1)S(1)} all-gather(bf16[256,768]{1,0:T(8,128)(2,1)S(1)} %multiply_convert_fusion.3), channel_id=1, replica_groups=mesh['dp'=16,'tensor'=2] {'tensor'}, dimensions={0}, use_global_device_ids=true | all-gather | bytes 1179648 | tf_op jit(solution)/shard_map/all_gather | solution.py:497
  38.6 1.2 multiply_convert_fusion.1
  40.5 0.8 fusion.23
  41.9 0.8 fusion.18
  42.7 0.8 select_bitcast_fusion
  43.5 2.9 %collective-permute-start.10 = (bf16[36,8,768]{2,1,0:T(8,128)(2,1)}, bf16[36,8,768]{2,1,0:T(8,128)(2,1)}, u32[]{:S(2)}, u32[]{:S(2)}) collective-permute-start(bf16[36,8,768]{2,1,0:T(8,128)(2,1)} %select_bitcast_fusion), channel_id=1, source_target_pairs={{0,4},{2,6},{4,0},{6,2},{8,12},{10,14},{12,8},{14,10},{16,20},{18,... | collective-permute-start | bytes 1327112 | tf_op jit(solution)/shard_map/ppermute | solution.py:20
  47.0 0.9 select_bitcast_fusion.1
  48.1 1.6 collective-permute-start.9
  49.7 0.8 convolution_add_fusion
  50.7 0.8 select_bitcast_fusion.2
  51.5 1.5 collective-permute-start.8
  53.8 1.0 collective-permute-done.6
  54.9 1.1 multiply_add_fusion
  55.9 2.6 %convolution_convert_fusion.5 = bf16[256,768]{1,0:T(8,128)(2,1)} fusion(bf16[384,768]{1,0:T(8,128)(2,1)S(1)} %copy-done.34, bf16[384,768]{1,0:T(8,128)(2,1)} %collective-permute-done.4, pred[]{:T(512)S(6)} %eq.49, f32[256,768]{1,0:T(8,128)S(1)} %get-tuple-element.61), kind=kOutput, calls=%fused_computation.22 | convolution fusion | flops 307691520 | bytes 2359297 | tf_op jit(solution)/shard_map/dot_general | solution.py:66
  59.6 1.2 bitcast_add_fusion.2
  60.8 1.1 bitcast_add_fusion.3
  61.9 2.5 %collective-permute-done.8 = bf16[36,8,768]{2,1,0:T(8,128)(2,1)} collective-permute-done((bf16[36,8,768]{2,1,0:T(8,128)(2,1)}, bf16[36,8,768]{2,1,0:T(8,128)(2,1)}, u32[]{:S(2)}, u32[]{:S(2)}) %collective-permute-start.8) | collective-permute-done | bytes 442400 | tf_op jit(solution)/shard_map/ppermute | solution.py:20
  64.4 1.1 bitcast_add_fusion.4
  65.4 0.7 broadcast_select_fusion
  66.2 1.5 collective-permute-start.13
  68.4 2.6 %collective-permute-start.12 = (bf16[18,8,768]{2,1,0:T(8,128)(2,1)}, bf16[18,8,768]{2,1,0:T(8,128)(2,1)}, u32[]{:S(2)}, u32[]{:S(2)}) collective-permute-start(bf16[18,8,768]{2,1,0:T(8,128)(2,1)} %broadcast_select_fusion.1), channel_id=1, source_target_pairs={{0,16},{2,18},{4,20},{6,22},{8,24},{10,26},{12,28},{14,30},{16,0},... | collective-permute-start | bytes 663560 | tf_op jit(solution)/shard_map/ppermute | solution.py:20
  72.2 1.9 copy.28
  74.1 1.2 fusion.35
  75.4 4.1 %convolution_bitcast_fusion = f32[512,12,64]{0,2,1:T(8,128)S(1)} fusion(bf16[256,12,64]{0,2,1:T(8,128)(2,1)} %bitcast.102, f32[12,256,512]{2,1,0:T(8,128)} %copy-done.1, f32[12,256]{1,0:T(8,128)} %copy-done.22), kind=kOutput, calls=%fused_computation.14 | convolution fusion | flops 206045184 | bytes 8269824 | tf_op jit(solution)/shard_map/hqk,qhd->khd/dot_general | solution.py:539
  79.6 4.2 %multiply_convert_fusion = bf16[12,256,512]{2,1,0:T(8,128)(2,1)S(1)} fusion(f32[12,256,512]{2,1,0:T(8,128)} %copy-done.1, f32[12,256]{1,0:T(8,128)S(1)} %fusion.35, f32[12,256]{1,0:T(8,128)S(1)} %copy-done.23, bf16[256,12,64]{0,2,1:T(8,128)(2,1)S(1)} %bitcast.103, bf16[256,12,64]{0,2,1:T(8,128)(2,1)S(1)} %bitcast.114, bf16[256,12,64]{0,2,1:T(8,128)(2,1)S(1)} %bitcast.116, ...), kind=kOutput, calls=%fused_computation | convolution fusion | flops 212729856 | bytes 10641409 | tf_op jit(solution)/shard_map/qhd,khd->hqk/dot_general | solution.py:530
  84.0 1.0 select_add_fusion
  85.1 1.0 select_add_fusion.1
  86.0 1.0 select_add_fusion.2
  87.9 2.4 %fusion.3 = f32[256,12,64]{0,2,1:T(8,128)S(1)} fusion(bf16[12,256,512]{2,1,0:T(8,128)(2,1)S(1)} %multiply_convert_fusion, bf16[256,12,64]{0,2,1:T(8,128)(2,1)} %maximum_convert_fusion, bf16[256,12,64]{0,2,1:T(8,128)(2,1)} %bitcast.7, pred[]{:T(512)S(6)} %eq.48), kind=kOutput, calls=%fused_computation.20 | convolution fusion | flops 205062144 | bytes 4718593 | tf_op jit(solution)/shard_map/hqk,khd->qhd/dot_general | solution.py:537
  91.5 1.6 collective-permute-start.16
  93.1 3.2 %collective-permute-done.18 = bf16[9,8,768]{2,1,0:T(8,128)(2,1)S(1)} collective-permute-done((bf16[9,8,768]{2,1,0:T(8,128)(2,1)S(1)}, bf16[9,8,768]{2,1,0:T(8,128)(2,1)S(1)}, u32[]{:S(2)}, u32[]{:S(2)}) %collective-permute-start.18) | collective-permute-done | bytes 110624 | tf_op jit(solution)/shard_map/ppermute | solution.py:20
  96.4 1.8 collective-permute-done.16
  98.9 0.8 copy-done.8
  99.8 3.1 %fusion.1.refs_0_ = bf16[96,8,2304]{2,1,0:T(8,128)(2,1)} fusion(bf16[256,768]{1,0:T(8,128)(2,1)S(1)} %copy-done.8, f32[768]{0:T(1024)S(1)} %copy-done.25, f32[256]{0:T(256)S(1)} %copy-done.30, f32[256]{0:T(256)S(1)} %copy-done.28, bf16[256,768]{0,1:T(8,128)(2,1)S(1)} %fusion.34, bf16[256,768]{0,1:T(8,128)(2,1)S(1)} %bitcast.112, ...), kind=kOutput, calls=%fused_computation.7 | convolution fusion | flops 912261120 | bytes 5116928 | tf_op jit(solution)/shard_map/dot_general | solution.py:72
  103.2 1.5 collective-permute-start.20
  104.7 2.6 %collective-permute-start.21 = (bf16[9,8,768]{2,1,0:T(8,128)(2,1)S(1)}, bf16[9,8,768]{2,1,0:T(8,128)(2,1)}, u32[]{:S(2)}, u32[]{:S(2)}) collective-permute-start(bf16[9,8,768]{2,1,0:T(8,128)(2,1)S(1)} %select_add_fusion.3), channel_id=1, source_target_pairs={{0,16},{2,18},{4,20},{6,22},{8,24},{10,26},{12,28},{14,30},{16,0},... | collective-permute-start | bytes 331784 | tf_op jit(solution)/shard_map/ppermute | solution.py:20
  107.3 3.5 %fusion.32 = (bf16[768]{0:T(1024)(128)(2,1)S(1)}, f32[256]{0:T(256)S(1)}, f32[256]{0:T(256)S(1)}, f32[256,768]{1,0:T(8,128)S(1)}) fusion(bf16[256,768]{1,0:T(8,128)(2,1)S(1)} %copy-done.8, f32[256]{0:T(256)S(1)} %copy-done.30, f32[256]{0:T(256)S(1)} %copy-done.28, f32[768]{0:T(1024)S(1)} %copy-done.25, bf16[256,2304]{0,1:T(8,128)(2,1)S(1)} %pad_maximum_fusion, ...), kind=kOutput, calls=%fused_computation.59 | convolution fusion | flops 923663104 | bytes 5906945 | tf_op jit(solution)/shard_map/dot_general | solution.py:66
  110.9 1.2 fusion.31
  112.1 1.1 collective-permute-done.19
  113.2 0.9 add.185
  114.1 0.9 add.186
  115.5 0.9 add.187
  116.4 75.3 %reduce_gradients.1 = (bf16[48,8,2304]{2,1,0:T(8,128)(2,1)S(1)}, bf16[48,8,768]{2,1,0:T(8,128)(2,1)S(1)}, bf16[1,8,768]{2,1,0:T(8,128)(2,1)S(1)}, bf16[216,8,768]{2,1,0:T(8,128)(2,1)S(1)}) custom-call(bf16[96,8,2304]{2,1,0:T(8,128)(2,1)S(1)} %copy-done, bf16[96,8,768]{2,1,0:T(8,128)(2,1)S(1)} %fusion.2.refs_1_, bf16[2,8,768]{2,1,0:T(8,128)(2,1)S(1)} %pad.4.refs_2_, ...), custom_call_target="tpu_custom_call" | custom-call | tf_op jit(solution)/shard_map/reduce_gradients/pallas_call | solution.py:415
  191.8 2.8 %convert_bitcast_fusion = f32[3,768,576]{1,2,0:T(8,128)} fusion(bf16[3,576,768]{2,1,0:T(8,128)(2,1)S(1)} %bitcast.100), kind=kLoop, calls=%fused_computation.4 | loop fusion | flops 1327104 | bytes 7962624 | tf_op jit(solution)/shard_map/transpose | solution.py:572
  194.6 2.0 %bitcast_convert_fusion = f32[384,2304]{1,0:T(8,128)} fusion(bf16[48,8,2304]{2,1,0:T(8,128)(2,1)S(1)} %get-tuple-element.36), kind=kLoop, calls=%fused_computation.9 | loop fusion | flops 884736 | bytes 5308416 | tf_op jit(solution)/shard_map/convert_element_type | solution.py:569
  196.6 1.1 bitcast_convert_fusion.1
  (148 shorter events, 14.0 us)
Async XLA Ops:
  0.6 7.1 %copy-start.31 = (bf16[384]{0:T(512)(128)(2,1)S(1)}, bf16[384]{0:T(512)(128)(2,1)}, u32[]{:S(2)}) copy-start(bf16[384]{0:T(512)(128)(2,1)} %param.8) | copy-start | bytes 2308
  0.6 7.1 %copy-start.7 = (bf16[256,768]{1,0:T(8,128)(2,1)S(1)}, bf16[256,768]{1,0:T(8,128)(2,1)}, u32[]{:S(2)}) copy-start(bf16[256,768]{1,0:T(8,128)(2,1)} %param.7) | copy-start | bytes 1179652
  0.7 7.1 %collective-permute-start.1 = (bf16[384,2304]{1,0:T(8,128)(2,1)}, bf16[384,2304]{1,0:T(8,128)(2,1)}, u32[]{:S(2)}, u32[]{:S(2)}) collective-permute-start(bf16[384,2304]{1,0:T(8,128)(2,1)} %param.9), channel_id=1, source_target_pairs={{0,1},{1,0},{2,3},{3,2},{4,5},{5,4},{6,7},{7,6},{8,9},{9,8},{10,11... | collective-permute-start | bytes 5308424 | tf_op jit(solution)/shard_map/ppermute | solution.py:20
  1.2 6.5 %collective-permute-start = (bf16[384]{0:T(512)(128)(2,1)}, bf16[384]{0:T(512)(128)(2,1)S(1)}, u32[]{:S(2)}, u32[]{:S(2)}) collective-permute-start(bf16[384]{0:T(512)(128)(2,1)} %param.8), channel_id=1, source_target_pairs={{0,1},{1,0},{2,3},{3,2},{4,5},{5,4},{6,7},{7,6},{8,9},{9,8},{10,11... | collective-permute-start | bytes 2312 | tf_op jit(solution)/shard_map/ppermute | solution.py:20
  1.3 31.5 %collective-permute-start.4 = (bf16[384,768]{1,0:T(8,128)(2,1)}, bf16[384,768]{1,0:T(8,128)(2,1)}, u32[]{:S(2)}, u32[]{:S(2)}) collective-permute-start(bf16[384,768]{1,0:T(8,128)(2,1)} %param.10), channel_id=1, source_target_pairs={{0,1},{1,0},{2,3},{3,2},{4,5},{5,4},{6,7},{7,6},{8,9},{9,8},{10,11... | collective-permute-start | bytes 1769480 | tf_op jit(solution)/shard_map/ppermute | solution.py:20
  1.7 16.7 %collective-permute-start.5 = (bf16[384]{0:T(512)(128)(2,1)}, bf16[384]{0:T(512)(128)(2,1)}, u32[]{:S(2)}, u32[]{:S(2)}) collective-permute-start(bf16[384]{0:T(512)(128)(2,1)} %param.11), channel_id=1, source_target_pairs={{0,1},{1,0},{2,3},{3,2},{4,5},{5,4},{6,7},{7,6},{8,9},{9,8},{10,11... | collective-permute-start | bytes 2312 | tf_op jit(solution)/shard_map/ppermute | solution.py:20
  3.0 8.8 %copy-start.27 = (f32[256]{0:T(256)}, f32[256]{0:T(256)S(1)}, u32[]{:S(2)}) copy-start(f32[256]{0:T(256)S(1)} %broadcast_multiply_fusion.5) | copy-start | bytes 3076
  4.2 7.6 %copy-start.29 = (f32[256]{0:T(256)}, f32[256]{0:T(256)S(1)}, u32[]{:S(2)}) copy-start(f32[256]{0:T(256)S(1)} %add_rsqrt_fusion.1) | copy-start | bytes 3076
  7.7 4.1 %copy-start.24 = (f32[768]{0:T(1024)}, f32[768]{0:T(1024)S(1)}, u32[]{:S(2)}) copy-start(f32[768]{0:T(1024)S(1)} %fusion.49) | copy-start | bytes 9220
  11.8 1.4 copy-start.12
  14.4 4.0 %copy-start.32 = (bf16[384]{0:T(512)(128)(2,1)S(1)}, bf16[384]{0:T(512)(128)(2,1)}, u32[]{:S(2)}) copy-start(bf16[384]{0:T(512)(128)(2,1)} %param.11) | copy-start | bytes 2308
  15.2 6.7 %collective-permute-start.3 = (bf16[256,768]{0,1:T(8,128)(2,1)}, bf16[256,768]{0,1:T(8,128)(2,1)}, u32[]{:S(2)}, u32[]{:S(2)}) collective-permute-start(bf16[256,768]{0,1:T(8,128)(2,1)} %bitcast.6), channel_id=1, source_target_pairs={{0,1},{1,0},{2,3},{3,2},{4,5},{5,4},{6,7},{7,6},{8,9},{9,8},{10,11... | collective-permute-start | bytes 1179656 | tf_op jit(solution)/shard_map/ppermute | solution.py:20
  18.4 3.3 %copy-start.16 = (f32[256,32]{0,1:T(8,128)S(1)}, f32[256,32]{0,1:T(8,128)}, u32[]{:S(2)}) copy-start(f32[256,32]{0,1:T(8,128)} %get-tuple-element.65) | copy-start | bytes 98308
  18.4 3.3 %copy-start.17 = (f32[256,32]{0,1:T(8,128)S(1)}, f32[256,32]{0,1:T(8,128)}, u32[]{:S(2)}) copy-start(f32[256,32]{0,1:T(8,128)} %get-tuple-element.66) | copy-start | bytes 98308
  20.3 6.8 %collective-permute-start.2 = (bf16[256,768]{1,0:T(8,128)(2,1)S(1)}, bf16[256,768]{1,0:T(8,128)(2,1)}, u32[]{:S(2)}, u32[]{:S(2)}) collective-permute-start(bf16[256,768]{1,0:T(8,128)(2,1)S(1)} %slice.328), channel_id=1, source_target_pairs={{0,1},{1,0},{2,3},{3,2},{4,5},{5,4},{6,7},{7,6},{8,9},{9,8},{10,11... | collective-permute-start | bytes 1179656 | tf_op jit(solution)/shard_map/ppermute | solution.py:20
  21.9 2.6 %copy-start.10 = (bf16[256,12,32]{0,2,1:T(8,128)(2,1)}, bf16[256,12,32]{0,2,1:T(8,128)(2,1)S(1)}, u32[]{:S(2)}) copy-start(bf16[256,12,32]{0,2,1:T(8,128)(2,1)S(1)} %get-tuple-element.60) | copy-start | bytes 589828
  24.4 2.7 %copy-start.1 = (f32[12,256,512]{2,1,0:T(8,128)}, f32[12,256,512]{2,1,0:T(8,128)S(1)}, u32[]{:S(2)}) copy-start(f32[12,256,512]{2,1,0:T(8,128)S(1)} %get-tuple-element.68) | copy-start | bytes 18874372
  24.4 3.9 %copy-start.18 = (bf16[256,768]{0,1:T(8,128)(2,1)S(1)}, bf16[256,768]{0,1:T(8,128)(2,1)}, u32[]{:S(2)}) copy-start(bf16[256,768]{0,1:T(8,128)(2,1)} %copy.25) | copy-start | bytes 1179652
  27.1 5.6 %copy-start.22 = (f32[12,256]{1,0:T(8,128)}, f32[12,256]{1,0:T(8,128)S(1)}, u32[]{:S(2)}) copy-start(f32[12,256]{1,0:T(8,128)S(1)} %log_add_fusion) | copy-start | bytes 36868
  28.3 4.5 %copy-start.20 = (bf16[256,768]{0,1:T(8,128)(2,1)}, bf16[256,768]{0,1:T(8,128)(2,1)S(1)}, u32[]{:S(2)}) copy-start(bf16[256,768]{0,1:T(8,128)(2,1)S(1)} %copy.24) | copy-start | bytes 1179652
  28.3 4.5 %copy-start.34 = (bf16[384,768]{1,0:T(8,128)(2,1)S(1)}, bf16[384,768]{1,0:T(8,128)(2,1)}, u32[]{:S(2)}) copy-start(bf16[384,768]{1,0:T(8,128)(2,1)} %param.10) | copy-start | bytes 1769476
  32.7 26.4 %copy-start.13 = (bf16[12,64,256]{2,1,0:T(8,128)(2,1)}, bf16[12,64,256]{2,1,0:T(8,128)(2,1)S(1)}, u32[]{:S(2)}) copy-start(bf16[12,64,256]{2,1,0:T(8,128)(2,1)S(1)} %convolution_convert_fusion.6) | copy-start | bytes 1179652
  34.8 3.1 %copy-start.9 = (bf16[3,768,576]{1,2,0:T(8,128)(2,1)S(1)}, bf16[3,768,576]{1,2,0:T(8,128)(2,1)}, u32[]{:S(2)}) copy-start(bf16[3,768,576]{1,2,0:T(8,128)(2,1)} %param.12) | copy-start | bytes 7962628
  35.2 3.4 %copy-start.15 = (f32[512,576]{0,1:T(8,128)S(1)}, f32[512,576]{0,1:T(8,128)}, u32[]{:S(2)}) copy-start(f32[512,576]{0,1:T(8,128)} %fusion.16) | copy-start | bytes 3538948
  40.4 10.2 %copy-start.3 = (bf16[576,768]{1,0:T(8,128)(2,1)}, bf16[576,768]{1,0:T(8,128)(2,1)S(1)}, u32[]{:S(2)}) copy-start(bf16[576,768]{1,0:T(8,128)(2,1)S(1)} %convolution_convert_fusion.4) | copy-start | bytes 2654212
  43.5 16.1 %collective-permute-start.10 = (bf16[36,8,768]{2,1,0:T(8,128)(2,1)}, bf16[36,8,768]{2,1,0:T(8,128)(2,1)}, u32[]{:S(2)}, u32[]{:S(2)}) collective-permute-start(bf16[36,8,768]{2,1,0:T(8,128)(2,1)} %select_bitcast_fusion), channel_id=1, source_target_pairs={{0,4},{2,6},{4,0},{6,2},{8,12},{10,14},{12,8},{14,10},{16,20},{18,... | collective-permute-start | bytes 1327112 | tf_op jit(solution)/shard_map/ppermute | solution.py:20
  47.0 1.1 copy-start.5
  48.1 12.7 %collective-permute-start.9 = (bf16[36,8,768]{2,1,0:T(8,128)(2,1)}, bf16[36,8,768]{2,1,0:T(8,128)(2,1)}, u32[]{:S(2)}, u32[]{:S(2)}) collective-permute-start(bf16[36,8,768]{2,1,0:T(8,128)(2,1)} %select_bitcast_fusion.1), channel_id=1, source_target_pairs={{0,8},{2,10},{4,12},{6,14},{8,0},{10,2},{12,4},{14,6},{16,24},{18,... | collective-permute-start | bytes 1327112 | tf_op jit(solution)/shard_map/ppermute | solution.py:20
  50.6 2.8 %collective-permute-start.7 = (bf16[256,768]{1,0:T(8,128)(2,1)S(1)}, bf16[256,768]{1,0:T(8,128)(2,1)S(1)}, u32[]{:S(2)}, u32[]{:S(2)}) collective-permute-start(bf16[256,768]{1,0:T(8,128)(2,1)S(1)} %select_convert_fusion.2), channel_id=1, source_target_pairs={{0,1},{1,0},{2,3},{3,2},{4,5},{5,4},{6,7},{7,6},{8,9},{9,8},{10,11... | collective-permute-start | bytes 1179656 | tf_op jit(solution)/shard_map/ppermute | solution.py:20
  51.5 12.9 %collective-permute-start.8 = (bf16[36,8,768]{2,1,0:T(8,128)(2,1)}, bf16[36,8,768]{2,1,0:T(8,128)(2,1)}, u32[]{:S(2)}, u32[]{:S(2)}) collective-permute-start(bf16[36,8,768]{2,1,0:T(8,128)(2,1)} %select_bitcast_fusion.2), channel_id=1, source_target_pairs={{0,2},{2,0},{4,6},{6,4},{8,10},{10,8},{12,14},{14,12},{16,18},{18,... | collective-permute-start | bytes 1327112 | tf_op jit(solution)/shard_map/ppermute | solution.py:20
  53.1 1.8 copy-start.14
  53.1 1.8 collective-permute-start.6
  59.1 1.7 copy-start.6
  59.6 4.8 %copy-start.4 = (bf16[576,768]{1,0:T(8,128)(2,1)S(1)}, bf16[576,768]{1,0:T(8,128)(2,1)}, u32[]{:S(2)}) copy-start(bf16[576,768]{1,0:T(8,128)(2,1)} %copy-done.3) | copy-start | bytes 2654212
  66.2 17.9 %collective-permute-start.13 = (bf16[18,8,768]{2,1,0:T(8,128)(2,1)}, bf16[18,8,768]{2,1,0:T(8,128)(2,1)}, u32[]{:S(2)}, u32[]{:S(2)}) collective-permute-start(bf16[18,8,768]{2,1,0:T(8,128)(2,1)} %broadcast_select_fusion), channel_id=1, source_target_pairs={{0,2},{2,0},{4,6},{6,4},{8,10},{10,8},{12,14},{14,12},{16,18},{18,... | collective-permute-start | bytes 663560 | tf_op jit(solution)/shard_map/ppermute | solution.py:20
  68.4 16.7 %collective-permute-start.12 = (bf16[18,8,768]{2,1,0:T(8,128)(2,1)}, bf16[18,8,768]{2,1,0:T(8,128)(2,1)}, u32[]{:S(2)}, u32[]{:S(2)}) collective-permute-start(bf16[18,8,768]{2,1,0:T(8,128)(2,1)} %broadcast_select_fusion.1), channel_id=1, source_target_pairs={{0,16},{2,18},{4,20},{6,22},{8,24},{10,26},{12,28},{14,30},{16,0},... | collective-permute-start | bytes 663560 | tf_op jit(solution)/shard_map/ppermute | solution.py:20
  71.7 14.4 %collective-permute-start.11 = (bf16[18,8,768]{2,1,0:T(8,128)(2,1)}, bf16[18,8,768]{2,1,0:T(8,128)(2,1)}, u32[]{:S(2)}, u32[]{:S(2)}) collective-permute-start(bf16[18,8,768]{2,1,0:T(8,128)(2,1)} %broadcast_select_fusion.2), channel_id=1, source_target_pairs={{0,4},{2,6},{4,0},{6,2},{8,12},{10,14},{12,8},{14,10},{16,20},{18,... | collective-permute-start | bytes 663560 | tf_op jit(solution)/shard_map/ppermute | solution.py:20
  75.3 4.2 %copy-start.2 = (bf16[256,768]{0,1:T(8,128)(2,1)S(1)}, bf16[256,768]{0,1:T(8,128)(2,1)}, u32[]{:S(2)}) copy-start(bf16[256,768]{0,1:T(8,128)(2,1)} %copy.28) | copy-start | bytes 1179652
  75.3 4.2 %copy-start.19 = (bf16[256,768]{0,1:T(8,128)(2,1)S(1)}, bf16[256,768]{0,1:T(8,128)(2,1)}, u32[]{:S(2)}) copy-start(bf16[256,768]{0,1:T(8,128)(2,1)} %copy.25) | copy-start | bytes 1179652
  75.3 4.2 %copy-start.21 = (bf16[256,768]{0,1:T(8,128)(2,1)S(1)}, bf16[256,768]{0,1:T(8,128)(2,1)}, u32[]{:S(2)}) copy-start(bf16[256,768]{0,1:T(8,128)(2,1)} %copy-done.20) | copy-start | bytes 1179652
  75.4 4.2 %copy-start.23 = (f32[12,256]{1,0:T(8,128)S(1)}, f32[12,256]{1,0:T(8,128)}, u32[]{:S(2)}) copy-start(f32[12,256]{1,0:T(8,128)} %copy-done.22) | copy-start | bytes 36868
  83.8 14.4 %collective-permute-start.15 = (bf16[256,768]{0,1:T(8,128)(2,1)S(1)}, bf16[256,768]{0,1:T(8,128)(2,1)S(1)}, u32[]{:S(2)}, u32[]{:S(2)}) collective-permute-start(bf16[256,768]{0,1:T(8,128)(2,1)S(1)} %bitcast.117), channel_id=1, source_target_pairs={{0,1},{1,0},{2,3},{3,2},{4,5},{5,4},{6,7},{7,6},{8,9},{9,8},{10,11... | collective-permute-start | bytes 1179656 | tf_op jit(solution)/shard_map/ppermute | solution.py:20
  84.0 3.0 %copy-start.11 = (bf16[256,12,32]{0,2,1:T(8,128)(2,1)S(1)}, bf16[256,12,32]{0,2,1:T(8,128)(2,1)}, u32[]{:S(2)}) copy-start(bf16[256,12,32]{0,2,1:T(8,128)(2,1)} %copy-done.10) | copy-start | bytes 589828
  90.3 6.0 %collective-permute-start.18 = (bf16[9,8,768]{2,1,0:T(8,128)(2,1)S(1)}, bf16[9,8,768]{2,1,0:T(8,128)(2,1)S(1)}, u32[]{:S(2)}, u32[]{:S(2)}) collective-permute-start(bf16[9,8,768]{2,1,0:T(8,128)(2,1)S(1)} %broadcast_select_fusion.4), channel_id=1, source_target_pairs={{0,8},{2,10},{4,12},{6,14},{8,0},{10,2},{12,4},{14,6},{16,24},{18,... | collective-permute-start | bytes 331784 | tf_op jit(solution)/shard_map/ppermute | solution.py:20
  90.9 5.5 %collective-permute-start.17 = (bf16[9,8,768]{2,1,0:T(8,128)(2,1)S(1)}, bf16[9,8,768]{2,1,0:T(8,128)(2,1)S(1)}, u32[]{:S(2)}, u32[]{:S(2)}) collective-permute-start(bf16[9,8,768]{2,1,0:T(8,128)(2,1)S(1)} %broadcast_select_fusion.3), channel_id=1, source_target_pairs={{0,2},{2,0},{4,6},{6,4},{8,10},{10,8},{12,14},{14,12},{16,18},{18,... | collective-permute-start | bytes 331784 | tf_op jit(solution)/shard_map/ppermute | solution.py:20
  91.5 6.7 %collective-permute-start.16 = (bf16[9,8,768]{2,1,0:T(8,128)(2,1)S(1)}, bf16[9,8,768]{2,1,0:T(8,128)(2,1)S(1)}, u32[]{:S(2)}, u32[]{:S(2)}) collective-permute-start(bf16[9,8,768]{2,1,0:T(8,128)(2,1)S(1)} %broadcast_select_fusion.5), channel_id=1, source_target_pairs={{0,8},{2,10},{4,12},{6,14},{8,0},{10,2},{12,4},{14,6},{16,24},{18,... | collective-permute-start | bytes 331784 | tf_op jit(solution)/shard_map/ppermute | solution.py:20
  93.1 5.2 %collective-permute-start.14 = (bf16[256,768]{0,1:T(8,128)(2,1)S(1)}, bf16[256,768]{0,1:T(8,128)(2,1)S(1)}, u32[]{:S(2)}, u32[]{:S(2)}) collective-permute-start(bf16[256,768]{0,1:T(8,128)(2,1)S(1)} %bitcast.118), channel_id=1, source_target_pairs={{0,1},{1,0},{2,3},{3,2},{4,5},{5,4},{6,7},{7,6},{8,9},{9,8},{10,11... | collective-permute-start | bytes 1179656 | tf_op jit(solution)/shard_map/ppermute | solution.py:20
  98.8 1.0 copy-start.8
  98.8 1.0 copy-start.25
  98.8 1.0 copy-start.28
  98.8 1.0 copy-start.30
  99.8 7.5 %copy-start.33 = (bf16[384,2304]{1,0:T(8,128)(2,1)S(1)}, bf16[384,2304]{1,0:T(8,128)(2,1)}, u32[]{:S(2)}) copy-start(bf16[384,2304]{1,0:T(8,128)(2,1)} %param.9) | copy-start | bytes 5308420
  102.9 10.3 %collective-permute-start.19 = (bf16[9,8,768]{2,1,0:T(8,128)(2,1)S(1)}, bf16[9,8,768]{2,1,0:T(8,128)(2,1)}, u32[]{:S(2)}, u32[]{:S(2)}) collective-permute-start(bf16[9,8,768]{2,1,0:T(8,128)(2,1)S(1)} %select_add_fusion.5), channel_id=1, source_target_pairs={{0,16},{2,18},{4,20},{6,22},{8,24},{10,26},{12,28},{14,30},{16,0},... | collective-permute-start | bytes 331784 | tf_op jit(solution)/shard_map/ppermute | solution.py:20
  103.2 10.9 %collective-permute-start.20 = (bf16[9,8,768]{2,1,0:T(8,128)(2,1)S(1)}, bf16[9,8,768]{2,1,0:T(8,128)(2,1)}, u32[]{:S(2)}, u32[]{:S(2)}) collective-permute-start(bf16[9,8,768]{2,1,0:T(8,128)(2,1)S(1)} %select_add_fusion.4), channel_id=1, source_target_pairs={{0,4},{2,6},{4,0},{6,2},{8,12},{10,14},{12,8},{14,10},{16,20},{18,... | collective-permute-start | bytes 331784 | tf_op jit(solution)/shard_map/ppermute | solution.py:20
  104.7 10.7 %collective-permute-start.21 = (bf16[9,8,768]{2,1,0:T(8,128)(2,1)S(1)}, bf16[9,8,768]{2,1,0:T(8,128)(2,1)}, u32[]{:S(2)}, u32[]{:S(2)}) collective-permute-start(bf16[9,8,768]{2,1,0:T(8,128)(2,1)S(1)} %select_add_fusion.3), channel_id=1, source_target_pairs={{0,16},{2,18},{4,20},{6,22},{8,24},{10,26},{12,28},{14,30},{16,0},... | collective-permute-start | bytes 331784 | tf_op jit(solution)/shard_map/ppermute | solution.py:20
  110.8 1.2 copy-start.26
  110.8 5.6 %copy-start = (bf16[96,8,2304]{2,1,0:T(8,128)(2,1)S(1)}, bf16[96,8,2304]{2,1,0:T(8,128)(2,1)}, u32[]{:S(2)}) copy-start(bf16[96,8,2304]{2,1,0:T(8,128)(2,1)} %fusion.1.refs_0_) | copy-start | bytes 10616836
